TPU v7x, 32 devices: a whole 2x2x4 slice. The times are simulated.
32 devices in a mesh: dp: 4 (over x, core), ctx: 4 (over z), tensor: 2 (over y).
Axes of the slice: x: 2, y: 2, z: 4, core: 2. Of those that a mesh axis runs over, the one named last changes fastest.
Arguments:
- inputs: bfloat16 [8192, 768], P(('dp', 'ctx')), may hold values from -6 to 6
- segments: int32 [4, 2048], P('dp', 'ctx'), may hold values from 0 to 7, never falling along the last dimension, each value on 1 to 1536 neighbouring positions
- query_proj: bfloat16 [768, 768], P(None, 'tensor'), may hold values from -0.4375 to 0.4375
- key_proj: bfloat16 [768, 768], P(None, 'tensor'), may hold values from -0.21875 to 0.21875
- value_proj: bfloat16 [768, 768], P(None, 'tensor'), may hold values from -0.21875 to 0.21875
- query_bias: bfloat16 [768], P('tensor'), may hold values from -3 to 3
- value_bias: bfloat16 [768], P('tensor'), may hold values from -0.59765625 to 0.59765625
- output_proj: bfloat16 [768, 768], P('tensor'), may hold values from -0.875 to 0.875
- output_bias: bfloat16 [768], replicated, may hold values from -1.1953125 to 1.1953125
- attn_gain: bfloat16 [768], replicated, may hold values from 0.5 to 1.5
- attn_shift: bfloat16 [768], replicated, may hold values from -1.1953125 to 1.1953125
- expand_proj: bfloat16 [768, 3072], P(None, 'tensor'), may hold values from -0.21875 to 0.21875
- expand_bias: bfloat16 [3072], P('tensor'), may hold values from -3 to 3
- shrink_proj: bfloat16 [3072, 768], P('tensor'), may hold values from -0.109375 to 0.109375
- shrink_bias: bfloat16 [768], replicated, may hold values from -1.1953125 to 1.1953125
- final_gain: bfloat16 [768], replicated, may hold values from 0.5 to 1.5
- final_shift: bfloat16 [768], replicated, may hold values from -1.1953125 to 1.1953125
- cotangent: bfloat16 [8192, 768], P(('dp', 'ctx')), may hold values from -6 to 6
Outputs:
- output: bfloat16 [8192, 768], P(('dp', 'ctx'))
- input_grad: float32 [8192, 768], P(('dp', 'ctx'))
- query_grad: float32 [768, 768], P(None, 'tensor')
- key_grad: float32 [768, 768], P(None, 'tensor')
- value_grad: float32 [768, 768], P(None, 'tensor')
- qbias_grad: float32 [768], P('tensor')
- vbias_grad: float32 [768], P('tensor')
- oproj_grad: float32 [768, 768], P('tensor')
- obias_grad: float32 [768], replicated
- again_grad: float32 [768], replicated
- ashift_grad: float32 [768], replicated
- expand_grad: float32 [768, 3072], P(None, 'tensor')
- ebias_grad: float32 [3072], P('tensor')
- shrink_grad: float32 [3072, 768], P('tensor')
- sbias_grad: float32 [768], replicated
- fgain_grad: float32 [768], replicated
- fshift_grad: float32 [768], replicated
Inputs may be any that keep to these rules, and one draw needn't show every extreme that they name: `segments`: along each sequence the ids never fall; every id from 0 to 7 names one document of the sequence, and one document has 1536 tokens.
All inputs are finite; a program needn't handle non-finite values.
Results may differ from a plain program's by a relative error of at most 0.019.
Values may be sent and summed in bfloat16 or wider, within the bound.
A program may use at most 256 MiB of HBM per device.

v0:
```python
import jax
import jax.numpy as jnp
from jax import lax
from jax.sharding import PartitionSpec as P

HEAD_DIM = 64


norm_eps = 1e-12
masked = -1e30
contract_rows = (((0,), (0,)), ((), ()))
contract_cols = (((1,), (1,)), ((), ()))


def matmul(left, right):
    return jnp.dot(left, right, preferred_element_type=jnp.float32)


def inner_rows(left, right):
    return lax.dot_general(left, right, contract_rows, preferred_element_type=jnp.float32)


def inner_cols(left, right):
    return lax.dot_general(left, right, contract_cols, preferred_element_type=jnp.float32)


def norm_forward(values, gain, shift):
    centred = values - jnp.mean(values, axis=-1, keepdims=True)
    spread = jnp.mean(centred * centred, axis=-1, keepdims=True)
    recip = lax.rsqrt(spread + norm_eps)
    normed = centred * recip
    return (normed * gain + shift, normed, recip)


def norm_backward(upstream, normed, recip, gain):
    scaled = upstream * gain
    centred = (
        scaled
        - jnp.mean(scaled, axis=-1, keepdims=True)
        - normed * jnp.mean(scaled * normed, axis=-1, keepdims=True)
    )
    return (centred * recip, jnp.sum(upstream * normed, axis=0), jnp.sum(upstream, axis=0))


def cross_scores(left, right):
    return inner_cols(left, right)


def spread_apply(weights_in, right):
    return matmul(weights_in, right)


def spread_transpose(weights_in, left):
    return inner_rows(weights_in, left)


def body(
    inputs,
    segments,
    query_proj,
    key_proj,
    value_proj,
    query_bias,
    value_bias,
    output_proj,
    output_bias,
    attn_gain,
    attn_shift,
    expand_proj,
    expand_bias,
    shrink_proj,
    shrink_bias,
    final_gain,
    final_shift,
    cotangent,
):
    head_count = query_proj.shape[1] // HEAD_DIM
    scale = HEAD_DIM ** (-0.5)
    seg_local = segments[0]
    queries = (matmul(inputs, query_proj) + query_bias.astype(jnp.float32)).astype(jnp.bfloat16)
    keys = matmul(inputs, key_proj).astype(jnp.bfloat16)
    values = (matmul(inputs, value_proj) + value_bias.astype(jnp.float32)).astype(jnp.bfloat16)
    all_keys, all_values, key_ids = (
        lax.all_gather(keys, "ctx", axis=0, tiled=True),
        lax.all_gather(values, "ctx", axis=0, tiled=True),
        lax.all_gather(seg_local.astype(jnp.bfloat16), "ctx", axis=0, tiled=True),
    )
    query_segs = seg_local.astype(jnp.float32)
    key_segs = key_ids.astype(jnp.float32)
    same_seg = query_segs[:, None] == key_segs[None, :]

    def split_heads(matrix):
        return jnp.swapaxes(matrix.reshape(matrix.shape[0], head_count, HEAD_DIM), 0, 1)

    def join_heads(stack):
        return jnp.swapaxes(stack, 0, 1).reshape(stack.shape[1], head_count * HEAD_DIM)

    query_heads = split_heads(queries)
    key_heads = split_heads(all_keys)
    value_heads = split_heads(all_values)

    def head_forward(state, triple):
        query_head, key_head, value_head = triple
        scores = cross_scores(query_head, key_head) * scale
        scores = jnp.where(same_seg, scores, masked)
        row_max = jnp.max(scores, axis=1, keepdims=True)
        exp_scores = jnp.where(same_seg, jnp.exp(scores - row_max), 0.0)
        row_sum = jnp.sum(exp_scores, axis=1, keepdims=True)
        attn_probs = (exp_scores / row_sum).astype(jnp.bfloat16)
        mixed = spread_apply(attn_probs, value_head)
        return (state, (mixed, row_max + jnp.log(row_sum)))

    mixed_heads, log_sums = lax.scan(head_forward, None, (query_heads, key_heads, value_heads))[1]
    attended = join_heads(mixed_heads).astype(jnp.bfloat16)
    attn_total = lax.psum(matmul(attended, output_proj).astype(jnp.bfloat16), "tensor").astype(
        jnp.float32
    )
    attn_gain_f = attn_gain.astype(jnp.float32)
    first, first_normed, first_recip = norm_forward(
        inputs.astype(jnp.float32) + attn_total + output_bias.astype(jnp.float32),
        attn_gain_f,
        attn_shift.astype(jnp.float32),
    )
    first_low = first.astype(jnp.bfloat16)
    pre_act = matmul(first_low, expand_proj) + expand_bias.astype(jnp.float32)
    activated, gelu_back = jax.vjp(lambda pre_in: jax.nn.gelu(pre_in, approximate=False), pre_act)
    hidden = activated.astype(jnp.bfloat16)
    feed_total = lax.psum(matmul(hidden, shrink_proj).astype(jnp.bfloat16), "tensor").astype(
        jnp.float32
    )
    second = first + feed_total + shrink_bias.astype(jnp.float32)
    final_gain_f = final_gain.astype(jnp.float32)
    output, second_normed, second_recip = norm_forward(
        second, final_gain_f, final_shift.astype(jnp.float32)
    )
    upstream = cotangent.astype(jnp.float32)
    grad_second, fgain_grad, fshift_grad = norm_backward(
        upstream, second_normed, second_recip, final_gain_f
    )
    sbias_grad = jnp.sum(grad_second, axis=0)
    grad_second_low = grad_second.astype(jnp.bfloat16)
    shrink_grad = inner_rows(hidden, grad_second_low)
    grad_act = inner_cols(grad_second_low, shrink_proj)
    grad_pre = gelu_back(grad_act)[0].astype(jnp.bfloat16)
    ebias_grad = jnp.sum(grad_pre.astype(jnp.float32), axis=0)
    expand_grad = inner_rows(first_low, grad_pre)
    grad_first = grad_second + lax.psum(
        inner_cols(grad_pre, expand_proj).astype(jnp.bfloat16), "tensor"
    ).astype(jnp.float32)
    grad_mix, again_grad, ashift_grad = norm_backward(
        grad_first, first_normed, first_recip, attn_gain_f
    )
    obias_grad = jnp.sum(grad_mix, axis=0)
    grad_mix_low = grad_mix.astype(jnp.bfloat16)
    oproj_grad = inner_rows(attended, grad_mix_low)
    grad_attended = inner_cols(grad_mix_low, output_proj).astype(jnp.bfloat16)
    grad_heads = split_heads(grad_attended)

    def head_backward(state, group):
        query_head, key_head, value_head, grad_head, log_sum = group
        scores = cross_scores(query_head, key_head) * scale
        attn_probs = jnp.where(same_seg, jnp.exp(scores - log_sum), 0.0)
        grad_probs = cross_scores(grad_head, value_head)
        row_dot = jnp.sum(attn_probs * grad_probs, axis=1, keepdims=True)
        grad_scores = (attn_probs * (grad_probs - row_dot)).astype(jnp.bfloat16)
        grad_query = spread_apply(grad_scores, key_head) * scale
        grad_key = spread_transpose(grad_scores, query_head) * scale
        grad_value = spread_transpose(attn_probs.astype(jnp.bfloat16), grad_head)
        return (state, (grad_query, grad_key, grad_value))

    query_back, key_back, value_back = lax.scan(
        head_backward, None, (query_heads, key_heads, value_heads, grad_heads, log_sums)
    )[1]
    grad_queries = join_heads(query_back).astype(jnp.bfloat16)
    key_sum, value_sum = (
        lax.psum_scatter(
            join_heads(key_back).astype(jnp.bfloat16), "ctx", scatter_dimension=0, tiled=True
        ).astype(jnp.float32),
        lax.psum_scatter(
            join_heads(value_back).astype(jnp.bfloat16), "ctx", scatter_dimension=0, tiled=True
        ).astype(jnp.float32),
    )
    grad_keys = key_sum.astype(jnp.bfloat16)
    grad_values = value_sum.astype(jnp.bfloat16)
    qbias_grad = jnp.sum(grad_queries.astype(jnp.float32), axis=0)
    vbias_grad = jnp.sum(grad_values.astype(jnp.float32), axis=0)
    query_grad = inner_rows(inputs, grad_queries)
    key_grad = inner_rows(inputs, grad_keys)
    value_grad = inner_rows(inputs, grad_values)
    back_terms = (
        inner_cols(grad_queries, query_proj)
        + inner_cols(grad_keys, key_proj)
        + inner_cols(grad_values, value_proj)
    )
    input_grad = grad_mix + lax.psum(back_terms.astype(jnp.bfloat16), "tensor").astype(jnp.float32)
    (
        query_grad,
        key_grad,
        value_grad,
        qbias_grad,
        vbias_grad,
        oproj_grad,
        obias_grad,
        again_grad,
        ashift_grad,
        expand_grad,
        ebias_grad,
        shrink_grad,
        sbias_grad,
        fgain_grad,
        fshift_grad,
    ) = lax.psum(
        (
            query_grad,
            key_grad,
            value_grad,
            qbias_grad,
            vbias_grad,
            oproj_grad,
            obias_grad,
            again_grad,
            ashift_grad,
            expand_grad,
            ebias_grad,
            shrink_grad,
            sbias_grad,
            fgain_grad,
            fshift_grad,
        ),
        ("dp", "ctx"),
    )
    return (
        output.astype(jnp.bfloat16),
        input_grad,
        query_grad,
        key_grad,
        value_grad,
        qbias_grad,
        vbias_grad,
        oproj_grad,
        obias_grad,
        again_grad,
        ashift_grad,
        expand_grad,
        ebias_grad,
        shrink_grad,
        sbias_grad,
        fgain_grad,
        fshift_grad,
    )


def solution(mesh):
    in_specs = (
        P(("dp", "ctx"), None),
        P("dp", "ctx"),
        P(None, "tensor"),
        P(None, "tensor"),
        P(None, "tensor"),
        P("tensor"),
        P("tensor"),
        P("tensor", None),
        P(),
        P(),
        P(),
        P(None, "tensor"),
        P("tensor"),
        P("tensor", None),
        P(),
        P(),
        P(),
        P(("dp", "ctx"), None),
    )
    out_specs = (
        P(("dp", "ctx"), None),
        P(("dp", "ctx"), None),
        P(None, "tensor"),
        P(None, "tensor"),
        P(None, "tensor"),
        P("tensor"),
        P("tensor"),
        P("tensor", None),
        P(),
        P(),
        P(),
        P(None, "tensor"),
        P("tensor"),
        P("tensor", None),
        P(),
        P(),
        P(),
    )
    return jax.shard_map(body, mesh=mesh, in_specs=in_specs, out_specs=out_specs, check_vma=False)
```

profile of v0, /device:TPU:0, one launch (start us, length us, event | category | flops | bytes accessed | tf_op | source)
XLA Modules:
  0.0 743.4 jit_solution(2113761524882374570)
XLA Ops:
  7.3 2.8 convolution_convert_fusion.4
  12.7 13.7 %all-gather = bf16[1,2048]{1,0:T(2,128)(2,1)S(1)} all-gather(bf16[1,512]{1,0:T(2,128)(2,1)S(1)} %get-tuple-element.288), channel_id=2, replica_groups=mesh['dp'=4,'ctx'=4,'tensor'=2] {'ctx'}, dimensions={1}, use_global_device_ids=true | all-gather | bytes 5120 | tf_op jit(solution)/shard_map/all_gather | solution.py:86
  29.1 21.0 %all-gather.4.cloned.1.call-done = bf16[2048,384]{1,0:T(8,128)(2,1)} async-done(((bf16[512,384]{1,0:T(8,128)(2,1)}), bf16[2048,384]{1,0:T(8,128)(2,1)}) %all-gather.4.cloned.1.call-update) | async-done | bytes 1572880 | tf_op jit(solution)/shard_map/all_gather | solution.py:84
  52.6 4.1 copy.45
  56.8 31.5 %all-gather.6.cloned.1.call-done = bf16[2048,384]{1,0:T(8,128)(2,1)} async-done(((bf16[512,384]{1,0:T(8,128)(2,1)}), bf16[2048,384]{1,0:T(8,128)(2,1)}) %all-gather.6.cloned.1.call-update) | async-done | bytes 1572880 | tf_op jit(solution)/shard_map/all_gather | solution.py:85
  90.8 4.1 copy.46
  94.9 38.4 %while.28 = (s32[]{:T(128)}, bf16[6,512,64]{1,2,0:T(8,128)(2,1)S(1)}, f32[6,512,1]{1,2,0:T(1,128)}, bf16[6,512,64]{2,1,0:T(8,128)(2,1)}, bf16[6,2048,64]{2,1,0:T...) while((s32[]{:T(128)}, ...), condition=%wide.region_3.4_spmd.clone, body=%wide.region_0.3_spmd.clone.sunk | while | flops 286260736 | bytes 13946985 | solution.py:113
  140.6 28.8 %all-reduce.8.cloned.1.call-done = bf16[512,768]{1,0:T(8,128)(2,1)} async-done(((bf16[512,768]{1,0:T(8,128)(2,1)}), bf16[512,768]{1,0:T(8,128)(2,1)}) %all-reduce.8.cloned.1.call-update) | async-done | bytes 786448 | tf_op jit(solution)/shard_map/psum | solution.py:115
  171.5 9.5 %multiply_convert_fusion.1 = (bf16[512,1536]{1,0:T(8,128)(2,1)S(1)}, f32[512,1536]{1,0:T(8,128)}, f32[512,1536]{1,0:T(8,128)}) fusion(f32[1536]{0:T(1024)S(1)} %copy-done.41, bf16[768,1536]{1,0:T(8,128)(2,1)S(1)} %copy-done, f32[768]{0:T(1024)S(1)} %copy-done.38, f32[768]{0:T(1024)S(1)} %copy-done.23, f32[512]{0:T(512)S(1)} %add_rsqrt_fusion.1, ...), kind=kOutput, calls=%fused_computation.62 | convolution fusion | flops 1263403008 | bytes 11815936 | tf_op jit(solution)/shard_map/dot_general | solution.py:16
  184.8 34.2 %all-reduce.10.cloned.1.call-done = bf16[512,768]{1,0:T(8,128)(2,1)} async-done(((bf16[512,768]{1,0:T(8,128)(2,1)}), bf16[512,768]{1,0:T(8,128)(2,1)}) %all-reduce.10.cloned.1.call-update) | async-done | bytes 786448 | tf_op jit(solution)/shard_map/psum | solution.py:128
  225.0 2.9 convert_reduce_fusion
  231.5 34.4 %all-reduce.12.cloned.1.call-done = bf16[512,768]{1,0:T(8,128)(2,1)} async-done(((bf16[512,768]{1,0:T(8,128)(2,1)}), bf16[512,768]{1,0:T(8,128)(2,1)}) %all-reduce.12.cloned.1.call-update) | async-done | bytes 786448 | tf_op jit(solution)/shard_map/psum | solution.py:147
  265.9 3.5 multiply_reduce_fusion.1
  273.7 70.0 %while.29 = (s32[]{:T(128)}, bf16[6,512,64]{1,2,0:T(8,128)(2,1)S(1)}, bf16[6,2048,64]{1,2,0:T(8,128)(2,1)}, bf16[6,2048,64]{1,2,0:T(8,128)(2,1)}, bf16[6,512,64]...) while((s32[]{:T(128)}, ...), condition=%wide.region_17.18_spmd.clone, body=%wide.region_15.17_spmd.clone.sunk | while | flops 681737728 | bytes 34759808 | solution.py:171
  345.1 5.1 fusion.67
  350.3 3.8 fusion.73
  357.4 21.8 %reduce-scatter.3.cloned.1.call-done = bf16[512,384]{0,1:T(8,128)(2,1)} async-done(((bf16[2048,384]{0,1:T(8,128)(2,1)}), bf16[512,384]{0,1:T(8,128)(2,1)}) %reduce-scatter.3.cloned.1.call-update) | async-done | bytes 393232 | tf_op jit(solution)/shard_map/reduce_scatter | solution.py:176
  379.1 3.0 fusion.82
  382.1 33.8 %reduce-scatter.5.cloned.1.call-done = bf16[512,384]{0,1:T(8,128)(2,1)} async-done(((bf16[2048,384]{0,1:T(8,128)(2,1)}), bf16[512,384]{0,1:T(8,128)(2,1)}) %reduce-scatter.5.cloned.1.call-update) | async-done | bytes 393232 | tf_op jit(solution)/shard_map/reduce_scatter | solution.py:179
  415.8 3.5 add_convert_fusion.1
  424.7 61.2 %all-reduce = (f32[384]{0:T(512)}, f32[384]{0:T(512)}, f32[768]{0:T(1024)}, f32[768]{0:T(1024)}, f32[768]{0:T(1024)}, /*index=5*/f32[1536]{0:T(1024)}, f32[768]{0:T(1024)}, f32[768]{0:T(1024)}, f32[768]{0:T(1024)}) all-reduce(f32[384]{0:T(512)S(1)} %reduce_sum.182, ...), channel_id=1, replica_groups=mesh['dp'=4,'ctx'=4,'tensor'=2] {'dp','ctx'}, use_global_device_ids=true, to_apply=%region_25.26 | all-reduce | flops 6912 | bytes 55296 | tf_op jit(solution)/shard_map/psum | solution.py:212
  488.3 231.7 %all-reduce.16.cloned.1.call-done = (f32[768,384]{0,1:T(8,128)}, f32[768,384]{0,1:T(8,128)}, f32[768,384]{0,1:T(8,128)}, f32[384,768]{1,0:T(8,128)}, f32[768,1536]{1,0:T(8,128)}, /*index=5*/f32[1536,768]{1,0:T(8,128)}) async-done(((f32[768,384]{0,1:T(8,128)}, f32[768,384]{0,1:T(8,128)}, f32[768,384]{0,1:T(8,128)}, f32[384,768]{1,0:T(8,128)}, f32[768,1536]{1,0:T(8,128)}, /*index=5*/f32[1536,768]{1,0:T(8,128)}), ...) | async-done | bytes 14155792 | tf_op jit(solution)/shard_map/psum | solution.py:212
  720.1 2.7 copy.50
  728.0 5.5 copy.92
  (259 shorter events, 166.2 us)
Async XLA Ops:
  7.2 164.2 %copy-start = (bf16[768,1536]{1,0:T(8,128)(2,1)S(1)}, bf16[768,1536]{1,0:T(8,128)(2,1)}, u32[]{:S(2)}) copy-start(bf16[768,1536]{1,0:T(8,128)(2,1)} %param.33) | copy-start | bytes 7077892
  7.2 42.8 %all-gather.4.cloned.1.call-start = ((), (), s32[]{:S(2)}) async-start(), calls=%async_computation.2 | async-start | bytes 1966080 | tf_op jit(solution)/shard_map/all_gather | solution.py:84
  10.1 78.1 %all-gather.6.cloned.1.call-start = ((), (), s32[]{:S(2)}) async-start(), calls=%async_computation.3 | async-start | bytes 1966080 | tf_op jit(solution)/shard_map/all_gather | solution.py:85
  12.6 156.8 %all-reduce.8.cloned.1.call-start = ((), (), s32[]{:S(2)}) async-start(), calls=%async_computation.4 | async-start | bytes 1572864 | tf_op jit(solution)/shard_map/psum | solution.py:115
  133.3 38.1 %copy-start.12 = (bf16[6,512,64]{1,2,0:T(8,128)(2,1)}, bf16[6,512,64]{1,2,0:T(8,128)(2,1)S(1)}, u32[]{:S(2)}) copy-start(bf16[6,512,64]{1,2,0:T(8,128)(2,1)S(1)} %get-tuple-element.109) | copy-start | bytes 1179652
  136.0 83.0 %all-reduce.10.cloned.1.call-start = ((), (), s32[]{:S(2)}) async-start(), calls=%async_computation.5 | async-start | bytes 1572864 | tf_op jit(solution)/shard_map/psum | solution.py:128
  170.9 10.1 %copy-start.26 = (f32[512]{0:T(512)}, f32[512]{0:T(512)S(1)}, u32[]{:S(2)}) copy-start(f32[512]{0:T(512)S(1)} %broadcast_multiply_fusion.5) | copy-start | bytes 6148
  171.5 9.6 %copy-start.29 = (f32[512]{0:T(512)}, f32[512]{0:T(512)S(1)}, u32[]{:S(2)}) copy-start(f32[512]{0:T(512)S(1)} %add_rsqrt_fusion.1) | copy-start | bytes 6148
  171.5 10.7 %copy-start.49 = (bf16[1536,768]{1,0:T(8,128)(2,1)S(1)}, bf16[1536,768]{1,0:T(8,128)(2,1)}, u32[]{:S(2)}) copy-start(bf16[1536,768]{1,0:T(8,128)(2,1)} %param.35) | copy-start | bytes 7077892
  182.2 36.8 %copy-start.24 = (f32[768]{0:T(1024)S(1)}, f32[768]{0:T(1024)}, u32[]{:S(2)}) copy-start(f32[768]{0:T(1024)} %convert_element_type.185) | copy-start | bytes 9220
  182.2 36.8 %copy-start.27 = (f32[512]{0:T(512)S(1)}, f32[512]{0:T(512)}, u32[]{:S(2)}) copy-start(f32[512]{0:T(512)} %copy-done.26) | copy-start | bytes 6148
  182.2 36.8 %copy-start.30 = (f32[512]{0:T(512)S(1)}, f32[512]{0:T(512)}, u32[]{:S(2)}) copy-start(f32[512]{0:T(512)} %copy-done.29) | copy-start | bytes 6148
  182.2 36.8 %copy-start.39 = (f32[768]{0:T(1024)S(1)}, f32[768]{0:T(1024)}, u32[]{:S(2)}) copy-start(f32[768]{0:T(1024)} %convert_element_type.186) | copy-start | bytes 9220
  184.5 81.4 %all-reduce.12.cloned.1.call-start = ((), (), s32[]{:S(2)}) async-start(), calls=%async_computation.6 | async-start | bytes 1572864 | tf_op jit(solution)/shard_map/psum | solution.py:147
  231.4 38.0 %copy-start.4 = (f32[512,768]{1,0:T(8,128)S(1)}, f32[512,768]{1,0:T(8,128)}, u32[]{:S(2)}) copy-start(f32[512,768]{1,0:T(8,128)} %copy-done.3) | copy-start | bytes 4718596
  231.4 38.0 %copy-start.9 = (bf16[512,768]{1,0:T(8,128)(2,1)S(1)}, bf16[512,768]{1,0:T(8,128)(2,1)}, u32[]{:S(2)}) copy-start(bf16[512,768]{1,0:T(8,128)(2,1)} %all-reduce.8.cloned.1.call-done) | copy-start | bytes 2359300
  231.4 147.7 %reduce-scatter.3.cloned.1.call-start = ((), (), s32[]{:S(2)}) async-start(), calls=%async_computation.7 | async-start | bytes 1966080 | tf_op jit(solution)/shard_map/reduce_scatter | solution.py:176
  343.7 72.2 %reduce-scatter.5.cloned.1.call-start = ((), (), s32[]{:S(2)}) async-start(), calls=%async_computation.8 | async-start | bytes 1966080 | tf_op jit(solution)/shard_map/reduce_scatter | solution.py:179
  344.4 5.8 copy-start.10
  344.4 5.8 copy-start.25
  344.5 141.4 %all-reduce.14.cloned.1.call-start = ((), (), s32[]{:S(2)}) async-start(), calls=%async_computation.9 | async-start | bytes 1572864 | tf_op jit(solution)/shard_map/psum | solution.py:195
  357.4 58.5 %copy-start.21 = (bf16[768,384]{1,0:T(8,128)(2,1)S(1)}, bf16[768,384]{1,0:T(8,128)(2,1)}, u32[]{:S(2)}) copy-start(bf16[768,384]{1,0:T(8,128)(2,1)} %param.26) | copy-start | bytes 1769476
  419.4 300.7 %all-reduce.16.cloned.1.call-start = ((), (), s32[]{:S(2)}) async-start(), calls=%async_computation.10 | async-start | bytes 28311552 | tf_op jit(solution)/shard_map/psum | solution.py:212
  727.0 6.5 slice-start
  (42 other events, 115.0 us)
Sparse Core Ops, SparseCore 0:
  10.2 39.8 all-gather.3
  52.2 35.9 all-gather.5
  136.1 33.1 all-reduce.7
  184.7 34.3 all-reduce.9
  231.5 34.3 all-reduce.11
  343.8 35.2 reduce-scatter.2
  381.5 34.2 reduce-scatter.4
  419.5 33.2 all-reduce.13
  459.1 260.8 all-reduce.15
where the time goes:
time: 746 us; the launch traced here: 743 us
  waiting for transfers between devices  438 us (59%)
  matrix products  141 us (19%)
  blocking collectives  74.9 us (10%)
  local copies, waits for them, and re-layouts  44.8 us (6%)
  other arithmetic  29.9 us (4%)
  between operations  14.4 us (2%)
    psum x1, waiting for transfers between devices, body(): lax.psum((query_grad, key_grad, value_grad, qbias_grad, vbias_grad, oproj...  232 us
    psum x1, blocking collectives, body(): lax.psum((query_grad, key_grad, value_grad, qbias_grad, vbias_grad, oproj...  61.2 us
    dot_general x24, matrix products, inner_cols(): lax.dot_general(left, right, contract_cols, preferred_element_type=jnp.fl...  52.3 us
    dot_general x18, matrix products, matmul(): return jnp.dot(left, right, preferred_element_type=jnp.float32)  47.6 us
    dot_general x18, matrix products, inner_rows(): lax.dot_general(left, right, contract_rows, preferred_element_type=jnp.fl...  40.7 us
    psum x1, waiting for transfers between devices, body(): lax.psum(inner_cols(grad_pre, expand_proj).astype(jnp.bfloat16), 'tensor')  34.4 us
    psum x1, waiting for transfers between devices, body(): lax.psum(matmul(hidden, shrink_proj).astype(jnp.bfloat16), 'tensor')  34.2 us
    reduce_scatter x1, waiting for transfers between devices, body(): lax.psum_scatter(join_heads(value_back).astype(jnp.bfloat16), 'ctx', scat...  33.8 us
  transfers between devices with their start and end apart: 9, of which 8 were waited for; matrix products, arithmetic and copies ran while one was open for 5% of the time, Pallas kernels for 0%

commit v1 on v0

--- a/solution.py
+++ b/solution.py
@@ -1,13 +1,840 @@
+import functools
+import types
+
 import jax
 import jax.numpy as jnp
 from jax import lax
+from jax.experimental import pallas as pl
+from jax.experimental.pallas import tpu as pltpu
 from jax.sharding import PartitionSpec as P
 
 HEAD_DIM = 64
-
-
 norm_eps = 1e-12
 masked = -1e30
+MESH = pl.DeviceIdType.MESH
+CORE, XS, YS, Z1, Z2 = range(5)
+BF16, F32 = jnp.bfloat16, jnp.float32
+INV_SQRT2 = 0.7071067811865476
+INV_SQRT_2PI = 0.3989422804014327
+
+
+def nn(left, right):
+    return jnp.dot(left, right, preferred_element_type=F32)
+
+
+def nt(left, right):
+    return lax.dot_general(left, right, (((1,), (1,)), ((), ())), preferred_element_type=F32)
+
+
+def tn(left, right):
+    return lax.dot_general(left, right, (((0,), (0,)), ((), ())), preferred_element_type=F32)
+
+
+def normalise(values):
+    centred = values - jnp.mean(values, axis=-1, keepdims=True)
+    spread = jnp.mean(centred * centred, axis=-1, keepdims=True)
+    recip = lax.rsqrt(spread + norm_eps)
+    return centred * recip, recip
+
+
+def denormalise(scaled, normed, recip):
+    return recip * (
+        scaled
+        - jnp.mean(scaled, axis=-1, keepdims=True)
+        - normed * jnp.mean(scaled * normed, axis=-1, keepdims=True)
+    )
+
+
+def gelu_parts(pre):
+    phi_sum = 0.5 + 0.5 * lax.erf(pre * INV_SQRT2)
+    slope = phi_sum + pre * (INV_SQRT_2PI * jnp.exp(-0.5 * pre * pre))
+    return pre * phi_sum, slope
+
+
+def column_sum(values):
+    return jnp.sum(values, axis=0, keepdims=True)
+
+
+class Shapes:
+    def __init__(self, mesh, tokens, width, heads_width, units):
+        self.nd, self.nc = mesh["dp"], mesh["ctx"]
+        self.nx = self.nd // 2
+        self.tokens, self.mine = tokens, tokens // 2
+        self.width, self.hw, self.units = width, heads_width, units
+        self.pairs = heads_width // 128
+
+
+def make_kernel(sh, names, orders):
+    T, TM, D, W, F = sh.tokens, sh.mine, sh.width, sh.hw, sh.units
+    HP = sh.pairs
+    TILE = 512
+    NTILE = F // TILE
+    SLOTS = 4
+    PARTS = 2
+    PR = TM // PARTS
+
+    def kernel(*refs):
+        r = types.SimpleNamespace(**dict(zip(names, refs)))
+        send_ref, recv_ref, local_ref = r.send, r.recv, r.local
+        d, c, t = lax.axis_index("dp"), lax.axis_index("ctx"), lax.axis_index("tensor")
+        core, xpos = lax.rem(d, 2), d // 2
+        low_bit, high_bit = lax.rem(c, 2), c // 2
+        next_c = c + 1 - 2 * low_bit
+        z1_peer, z2_peer = (d, next_c, t), (d, c + 2 - 4 * high_bit, t)
+        z3_peer = (d, next_c + 2 - 4 * high_bit, t)
+        y_peer = (d, c, 1 - t)
+        core_peer = (d + 1 - 2 * core, c, t)
+        x_peer = (d + 2 - 4 * xpos, c, t)
+        peer_of = {CORE: core_peer, XS: x_peer, YS: y_peer, Z1: z1_peer, Z2: z2_peer}
+        bit_of = {CORE: core, XS: xpos, YS: t, Z1: low_bit, Z2: high_bit}
+        my_rows = pl.ds(pl.multiple_of(t * TM, TM), TM)
+        peer_rows = pl.ds(pl.multiple_of((1 - t) * TM, TM), TM)
+        counts = [0, 0]
+
+        def take(kind, k=1):
+            at = counts[kind]
+            counts[kind] += k
+            assert counts[kind] <= (send_ref, local_ref)[kind].shape[0], counts
+            return at
+
+        def remote(src, dst, device, at=None):
+            at = take(0) if at is None else at
+            return pltpu.make_async_remote_copy(
+                src_ref=src, dst_ref=dst, send_sem=send_ref.at[at], recv_sem=recv_ref.at[at],
+                device_id=device, device_id_type=MESH,
+            )
+
+        def local(src, dst):
+            return pltpu.make_async_copy(src, dst, local_ref.at[take(1)])
+
+        unsent = []
+
+        def go(copy):
+            copy.start()
+            unsent.append(copy)
+
+        def wait_sends(*but):
+            for copy in unsent:
+                if not any(copy is other for other in but):
+                    copy.wait_send()
+            unsent[:] = but
+
+        loads = types.SimpleNamespace(
+            x=local(r.x_in, r.xall.at[0]),
+            wk=local(r.wk_in, r.wqkv.at[:, pl.ds(W, W)]),
+            wv=local(r.wv_in, r.wqkv.at[:, pl.ds(2 * W, W)]),
+            wq=local(r.wq_in, r.wqkv.at[:, pl.ds(0, W)]),
+            wo=local(r.wo_in, r.wo.at[pl.ds(0, W)]),
+            we=local(r.we_in, r.we.at[0]),
+            ws=local(r.ws_in, r.ws.at[0]),
+            cot=local(r.cot_in.at[my_rows], r.cot),
+        )
+        for copy in vars(loads).values():
+            copy.start()
+
+        def row(ref):
+            return ref[...].astype(F32).reshape(1, ref.shape[0])
+
+        vec = [row(ref) for ref in (r.ob_in, r.ag_in, r.as_in, r.sb_in, r.fg_in, r.fs_in)]
+        r.eb[0] = row(r.eb_in)
+        r.segs[0] = r.seg_in[...].astype(F32)
+        barrier = pltpu.get_barrier_semaphore()
+        greeted = [y_peer, core_peer, x_peer, z1_peer, z2_peer, z3_peer]
+        for device in greeted:
+            pl.semaphore_signal(barrier, inc=1, device_id=device, device_id_type=MESH)
+        pl.semaphore_wait(barrier, len(greeted))
+
+        seg_copies = [None] + [
+            remote(r.segs.at[0], r.segs.at[k], peer) for k, peer in ((1, z1_peer), (2, z2_peer), (3, z3_peer))
+        ]
+        eb_copy = remote(r.eb.at[0], r.eb.at[1], y_peer)
+        x_rows = [pl.ds(pl.multiple_of(t * TM + k * PR, PR), PR) for k in range(PARTS)]
+        x_z, x_y = {}, {}
+        for k in range(PARTS):
+            mine = x_rows[k]
+            x_z[1, k] = remote(r.x_in.at[mine], r.xall.at[1, mine], z1_peer)
+            x_z[2, k] = remote(r.x_in.at[mine], r.xall.at[2, mine], z2_peer)
+            x_z[3, k] = remote(r.xall.at[2, mine], r.xall.at[3, mine], z1_peer)
+            for slot in (1, 2, 3):
+                x_y[slot, k] = remote(r.xall.at[slot, mine], r.xall.at[slot, mine], y_peer)
+        for slot in (1, 2):
+            for k in range(PARTS):
+                go(x_z[slot, k])
+        for copy in seg_copies[1:]:
+            go(copy)
+        go(eb_copy)
+
+        def pass_on(slot, k):
+            x_z[slot, k].wait_recv()
+            go(x_y[slot, k])
+            if slot == 2:
+                go(x_z[3, k])
+
+        def block_here(slot):
+            seg_copies[slot].wait_recv()
+            for k in range(PARTS):
+                x_y[slot, k].wait_recv()
+
+        chunks = [
+            (r.wo_in, r.wo.at[pl.ds(W, W)], W, 0, 1),
+            (r.we_in, r.we.at[1], D, 0, 2),
+            (r.we_in, r.we.at[1], D, 1, 2),
+            (r.ws_in, r.ws.at[1], F, 0, 2),
+            (r.ws_in, r.ws.at[1], F, 1, 2),
+        ]
+        pieces = sh.nd * 2
+
+        def window(chunk, owner):
+            rows, part, parts = chunk[2:]
+            size = rows // pieces // parts
+            return pl.ds(pl.multiple_of(owner * (rows // pieces) + part * size, size), size)
+
+        own_piece, pair_piece = d * 2 + low_bit, d * 2 + 1 - low_bit
+        x_d = d + 2 - 4 * xpos
+        x_pieces = (x_d * 2 + low_bit, x_d * 2 + 1 - low_bit)
+        w_y, w_z, w_x, w_core = [], [], [], []
+        for chunk in chunks:
+            source, held = chunk[0], chunk[1]
+
+            def move(owner, peer):
+                where = window(chunk, owner)
+                return remote(held.at[where], held.at[where], peer)
+
+            own = window(chunk, own_piece)
+            w_y.append(remote(source.at[own], held.at[own], y_peer))
+            w_z.append(move(own_piece, z1_peer))
+            w_x.append([move(piece, x_peer) for piece in (own_piece, pair_piece)])
+            w_core.append([move(piece, core_peer) for piece in (own_piece, pair_piece) + x_pieces])
+
+        def hop1(i):
+            w_y[i].wait_recv()
+            go(w_z[i])
+            go(w_x[i][0])
+            go(w_core[i][0])
+
+        def hop2(i):
+            w_z[i].wait_recv()
+            go(w_x[i][1])
+            go(w_core[i][1])
+
+        def hop3(i):
+            for k in range(2):
+                w_x[i][k].wait_recv()
+                go(w_core[i][2 + k])
+
+        def weights_done(i):
+            for copy in w_core[i]:
+                copy.wait_recv()
+
+        for i in range(2):
+            go(w_y[i])
+
+        kv = r.kv
+        value_bias = row(r.vb_in)
+        scale = HEAD_DIM ** (-0.5)
+        lane = lax.broadcasted_iota(jnp.int32, (T, 128), 1)
+
+        def split_pair(target, p, pair):
+            target[2 * p] = jnp.where(lane < 64, pair, 0.0).astype(BF16)
+            target[2 * p + 1] = jnp.where(lane < 64, 0.0, pair).astype(BF16)
+
+        def set_keys_values(slot):
+            both = nn(r.xall[slot], r.wqkv[:, W:])
+            for p in range(HP):
+                kv[slot, p, 0] = both[:, p * 128 : (p + 1) * 128].astype(BF16)
+                cols = slice(W + p * 128, W + (p + 1) * 128)
+                kv[slot, p, 1] = (both[:, cols] + value_bias[:, p * 128 : (p + 1) * 128]).astype(BF16)
+
+        def set_bias(slot):
+            seg_keys = jnp.broadcast_to(r.segs[slot], (128, T)).T
+            for j in range(T // 128):
+                cols = slice(j * 128, (j + 1) * 128)
+                r.bias[:, cols] = jnp.where(seg_keys == r.segs[0, :, cols], 0.0, masked)
+
+        loads.x.wait()
+        loads.wk.wait()
+        loads.wv.wait()
+        set_keys_values(0)
+        loads.wq.wait()
+        queries = (nn(r.xall[0], r.wqkv[:, :W]) + row(r.qb_in)).astype(BF16).astype(F32) * scale
+        for p in range(HP):
+            split_pair(r.qm, p, queries[:, p * 128 : (p + 1) * 128])
+
+        m_s, l_s, acc = r.m_s, r.l_s, r.acc
+        m_s[...] = jnp.full_like(m_s, masked)
+        l_s[...] = jnp.zeros_like(l_s)
+        acc[...] = jnp.zeros_like(acc)
+
+        def attend(slot, p):
+            pair_keys = kv[slot, p, 0]
+            pair_values = kv[slot, p, 1].T
+            for hh in range(2):
+                h = 2 * p + hh
+                s = nt(pair_keys, r.qm[h]) + r.bias[...]
+                old = m_s[h]
+                new = jnp.maximum(old, jnp.max(s, axis=0, keepdims=True))
+                e = jnp.exp(s - new)
+                alpha = jnp.exp(old - new)
+                l_s[h] = l_s[h] * alpha + jnp.sum(e, axis=0, keepdims=True)
+                m_s[h] = new
+                acc[h] = acc[h] * alpha + nn(pair_values[hh * 64 : hh * 64 + 64], e.astype(BF16))
+
+        def run(body, services=None):
+            def step(p, carry):
+                body(p)
+                for at, fn in (services or {}).items():
+                    pl.when(p == at)(fn)
+                return carry
+
+            lax.fori_loop(0, HP, step, 0)
+
+        def together(*fns):
+            def all_of():
+                for fn, arg in fns:
+                    fn(*arg)
+
+            return all_of
+
+        set_bias(0)
+        run(lambda p: attend(0, p), {0: together((pass_on, (1, 0))), 2: together((pass_on, (1, 1)))})
+        hop1(0)
+        go(w_y[2])
+        for slot in (1, 2, 3):
+            if slot == 1:
+                r.xt[:, 0:T] = r.xall[0].T
+                block_here(1)
+                set_keys_values(1)
+                set_bias(1)
+                run(lambda p: attend(1, p), {0: together((pass_on, (2, 0))), 2: together((hop2, (0,)), (hop1, (1,)))})
+                pass_on(2, 1)
+                go(w_y[3])
+                r.xt[:, T : 2 * T] = r.xall[1].T
+            elif slot == 2:
+                block_here(2)
+                set_keys_values(2)
+                set_bias(2)
+                run(lambda p: attend(2, p), {0: together((hop2, (1,)), (hop3, (0,))), 2: together((pass_on, (3, 0)))})
+                hop1(2)
+                go(w_y[4])
+                r.xt[:, 2 * T : 3 * T] = r.xall[2].T
+                pass_on(3, 1)
+                hop3(1)
+                hop2(2)
+            else:
+                block_here(3)
+                set_keys_values(3)
+                set_bias(3)
+        att_at = take(0, HP)
+
+        def att_copy(p):
+            cols = pl.ds(p * 128, 128)
+            return remote(r.att.at[peer_rows, cols], r.att_o.at[:, cols], y_peer, att_at + p)
+
+        for p in range(HP):
+            attend(3, p)
+            for h in (2 * p, 2 * p + 1):
+                acc[h] = acc[h] / l_s[h]
+                m_s[h] = m_s[h] + jnp.log(l_s[h])
+            pair = acc[2 * p : 2 * p + 2].reshape(128, T).T
+            r.att[:, p * 128 : (p + 1) * 128] = pair.astype(BF16)
+            att_copy(p).start()
+            if p == 0:
+                hop1(3)
+            if p == 1:
+                hop3(2)
+        hop2(3)
+        loads.wo.wait()
+        weights_done(0)
+        loads.cot.wait()
+
+        mix = nn(r.att[my_rows, :], r.wo[0:W, :])
+        r.xt[:, 3 * T :] = r.xall[3].T
+        for p in range(HP):
+            att_copy(p).wait_recv()
+        mix = mix + nn(r.att_o[...], r.wo[W : 2 * W, :])
+        normed, recip = normalise(r.xall[0, my_rows, :].astype(F32) + mix + vec[0])
+        r.n1[...] = normed
+        r.r1[...] = jnp.broadcast_to(recip, (TM, 128))
+        first = normed * vec[1] + vec[2]
+        r.sec[...] = first + vec[3]
+        r.fl[my_rows, :] = first.astype(BF16)
+        fl_copy = remote(r.fl.at[my_rows], r.fl.at[my_rows], y_peer)
+        loads.we.wait()
+        loads.ws.wait()
+        hop1(4)
+        go(fl_copy)
+
+
+        def tile_cols(j):
+            return pl.ds(pl.multiple_of(j * TILE, TILE), TILE)
+
+        def forward_tile(side, j):
+            cols = tile_cols(j)
+            pre = nn(r.fl[my_rows, :], r.we[side, :, cols]) + r.eb[side, :, cols]
+            hidden, slope = gelu_parts(pre)
+            hidden = hidden.astype(BF16)
+            r.gp[side, :, cols] = slope
+            if side == 0:
+                r.hid[my_rows, cols] = hidden
+            r.sec[...] += nn(hidden, r.ws[side, cols, :])
+
+        def tiles(fn):
+            def step(j, carry):
+                fn(j)
+                return carry
+
+            lax.fori_loop(0, NTILE, step, 0)
+
+        tiles(lambda j: forward_tile(0, j))
+        hop3(3)
+        hop2(4)
+        eb_copy.wait_recv()
+        weights_done(1)
+        weights_done(2)
+        hop3(4)
+        weights_done(3)
+        weights_done(4)
+        tiles(lambda j: forward_tile(1, j))
+        normed2, recip2 = normalise(r.sec[...])
+        upstream = r.cot[...].astype(F32)
+        grad_second = denormalise(upstream * vec[4], normed2, recip2)
+        r.gf[...] = grad_second
+        r.gs[my_rows, :] = grad_second.astype(BF16)
+        gs_copy = remote(r.gs.at[my_rows], r.gs.at[my_rows], y_peer)
+        go(gs_copy)
+        small = r.small
+        small[0:1, :] = column_sum(upstream * normed2)
+        small[1:2, :] = column_sum(upstream)
+        small[2:3, :] = column_sum(grad_second)
+        r.oy[...] = (normed2 * vec[4] + vec[5]).astype(BF16)
+        oy_local = local(r.oy, r.out.at[my_rows])
+        oy_local.start()
+
+
+        def backward_tile(side, j):
+            cols = tile_cols(j)
+            low = (nt(r.gs[my_rows, :], r.ws[side, cols, :]) * r.gp[side, :, cols]).astype(BF16)
+            if side == 0:
+                r.gpre[my_rows, cols] = low
+            r.gf[...] += nt(low, r.we[side, :, cols])
+
+        tiles(lambda j: backward_tile(0, j))
+        tiles(lambda j: backward_tile(1, j))
+        grad_first = r.gf[...]
+        normed = r.n1[...]
+        grad_mix = denormalise(grad_first * vec[1], normed, r.r1[:, 0:1])
+        r.gmix[...] = grad_mix
+        r.gm[my_rows, :] = grad_mix.astype(BF16)
+        gm_copy = remote(r.gm.at[my_rows], r.gm.at[my_rows], y_peer)
+        go(gm_copy)
+        small[3:4, :] = column_sum(grad_first * normed)
+        small[4:5, :] = column_sum(grad_first)
+        small[5:6, :] = column_sum(grad_mix)
+
+        def rows_at(ref, first_row, rows):
+            return ref.at[pl.ds(pl.multiple_of(first_row, rows), rows)]
+
+        class Unit:
+            def __init__(self, grad, whole, out, order, bufs):
+                self.grad, self.whole, self.out, self.order, self.bufs = grad, whole, out, order, bufs
+                self.first, self.rows = [0], [grad.shape[0]]
+                for stage in order:
+                    self.rows.append(self.rows[-1] // 2)
+                    self.first.append(self.first[-1] + bit_of[stage] * self.rows[-1])
+                self.down, self.up = {}, {}
+
+            def send(self, k):
+                stage, rows = self.order[k], self.rows[k + 1]
+                theirs = self.first[k] + (1 - bit_of[stage]) * rows
+                self.down[k] = remote(rows_at(self.grad, theirs, rows), self.bufs[k], peer_of[stage])
+                go(self.down[k])
+
+            def add(self, k):
+                self.down[k].wait_recv()
+                rows, first_row = self.rows[k + 1], self.first[k + 1]
+                step = next(v for v in (96, 48) if rows % v == 0)
+
+                def tile(i, carry):
+                    window = self.grad.at[pl.ds(pl.multiple_of(first_row + i * step, step), step)]
+                    there = pl.ds(pl.multiple_of(i * step, step), step)
+                    window[...] = (window[...].astype(F32) + self.bufs[k][there, :].astype(F32)).astype(BF16)
+                    return carry
+
+                lax.fori_loop(0, rows // step, tile, 0)
+
+            def forward(self, k):
+                self.add(k)
+                self.send(k + 1)
+
+            def spread(self, k):
+                rows, first_row = self.rows[k + 1], self.first[k + 1]
+                target = rows_at(self.whole, first_row, rows)
+                last = k == len(self.order) - 1
+                source = rows_at(self.grad, first_row, rows) if last else target
+                self.up[k] = remote(source, target, peer_of[self.order[k]])
+                go(self.up[k])
+                if last:
+                    self.kept = local(source, target)
+                    self.kept.start()
+
+            def turn(self):
+                k = len(self.order) - 1
+                self.add(k)
+                self.spread(k)
+
+            def back(self, k):
+                if k == len(self.order) - 1:
+                    self.kept.wait()
+                self.up[k].wait_recv()
+                self.spread(k - 1)
+
+            def store(self):
+                self.up[0].wait_recv()
+                self.kept = local(self.whole, self.out)
+                self.kept.start()
+
+        def all_sum(buf, slots, stages):
+            copies = [remote(buf.at[k % 2], slots.at[k], peer_of[stage]) for k, stage in enumerate(stages)]
+
+            def start(k):
+                copies[k].start()
+
+            def finish(k):
+                copies[k].wait()
+                total = buf[k % 2] + slots[k]
+                if stages[k] == YS:
+                    which = lax.broadcasted_iota(jnp.int32, total.shape, 0)
+                    total = jnp.where(which < 6, total, buf[k % 2])
+                buf[(k + 1) % 2] = total
+                if k + 1 < len(stages):
+                    start(k + 1)
+
+            return start, finish
+
+        fl_copy.wait_recv()
+        gs_copy.wait_recv()
+
+        def other_tile(j):
+            cols = tile_cols(j)
+            pre = nn(r.fl[peer_rows, :], r.we[0, :, cols]) + r.eb[0, :, cols]
+            hidden, slope = gelu_parts(pre)
+            r.hid[peer_rows, cols] = hidden.astype(BF16)
+            r.gpre[peer_rows, cols] = (nt(r.gs[peer_rows, :], r.ws[0, cols, :]) * slope).astype(BF16)
+
+        tiles(other_tile)
+        wait_sends(gm_copy)
+        unit_s = Unit(r.ws.at[1], r.ws.at[0], r.us_out, orders[0], (r.us_r0, r.us_r1, r.us_r2, r.us_r3))
+        unit_e = Unit(r.we.at[1], r.we.at[0], r.ue_out, orders[1], (r.ue_r0, r.ue_r1, r.ue_r2, r.ue_r3))
+
+        def half_of(which):
+            return which * core + (1 - which) * (1 - core)
+
+        def shrink_tiles(which):
+            base = half_of(which) * (F // 2)
+
+            def tile(i, carry):
+                at = pl.multiple_of(base + i * 384, 128)
+                r.ws[1, pl.ds(at, 384), :] = tn(r.hid[:, pl.ds(at, 384)], r.gs[...]).astype(BF16)
+                return carry
+
+            lax.fori_loop(0, F // 2 // 384, tile, 0)
+
+        def half_rows(which):
+            return pl.ds(pl.multiple_of(half_of(which) * (D // 2), D // 2), D // 2)
+
+        def expand_tiles(which):
+            rows = half_rows(which)
+
+            def tile(j):
+                cols = tile_cols(j)
+                r.we[1, rows, cols] = nn(r.flt[rows, :], r.gpre[:, cols]).astype(BF16)
+
+            tiles(tile)
+
+        shrink_tiles(0)
+        unit_s.send(0)
+        r.flt[...] = r.fl[...].T
+        shrink_tiles(1)
+        expand_tiles(0)
+        unit_e.send(0)
+        unit_s.forward(0)
+        expand_tiles(1)
+        unit_e.forward(0)
+        totals = column_sum(r.gpre[...].astype(F32))
+        small[6:7, :] = totals[:, :D]
+        small[7:8, :] = totals[:, D:]
+        r.es[0] = small[...]
+        early_start, early_finish = all_sum(r.es, r.es_r, (YS, CORE, XS, Z1, Z2))
+        early_start(0)
+
+        gm_copy.wait_recv()
+        grad_att = nt(r.gm[...], r.wo[0:W, :]).astype(BF16).astype(F32)
+        flipped = grad_att.T.reshape(2 * HP, 64, T)
+        r.delta[...] = jnp.sum(acc[...] * flipped, axis=1, keepdims=True)
+        for p in range(HP):
+            split_pair(r.dm, p, grad_att[:, p * 128 : (p + 1) * 128])
+        acc[...] = jnp.zeros_like(acc)
+        oy_send = remote(r.oy, r.out.at[my_rows], y_peer)
+        dkv = r.dkv
+
+        def pull(slot, p):
+            pair_keys, pair_values = kv[slot, p, 0], kv[slot, p, 1]
+            flipped_keys = pair_keys.T
+            grad_k = jnp.zeros((T, 128), F32)
+            grad_v = jnp.zeros((T, 128), F32)
+            for hh in range(2):
+                h = 2 * p + hh
+                q, g = r.qm[h], r.dm[h]
+                probs = jnp.exp(nt(pair_keys, q) + (r.bias[...] - m_s[h]))
+                grad_p = nt(pair_values, g)
+                grad_v = grad_v + nn(probs.astype(BF16), g)
+                ds = (probs * (grad_p - r.delta[h])).astype(BF16)
+                grad_k = grad_k + nn(ds, q)
+                acc[h] += nn(flipped_keys[hh * 64 : hh * 64 + 64], ds)
+            rows = slice(slot * T, (slot + 1) * T)
+            dkv[rows, pl.ds(pl.multiple_of(p * 128, 128), 128)] = grad_k.astype(BF16)
+            dkv[rows, pl.ds(pl.multiple_of(W + p * 128, 128), 128)] = grad_v.astype(BF16)
+
+        dx_y = [remote(r.xall.at[k, pl.ds(0, TM)], r.dxy.at[k], y_peer) for k in range(SLOTS)]
+        dx_z = {
+            3: remote(r.xall.at[3, pl.ds(TM, TM)], r.dxz.at[0], z1_peer),
+            1: remote(r.xall.at[1, pl.ds(TM, TM)], r.dxz.at[1], z1_peer),
+            2: remote(r.xall.at[2, pl.ds(TM, TM)], r.dxz.at[2], z2_peer),
+        }
+
+        def dx_rows(slot, rows):
+            here = pl.ds(pl.multiple_of(slot * T + rows.start, TM), TM)
+            return nt(dkv[here, :], r.wqkv[:, W:])
+
+        def dx_part(slot):
+            r.xall[slot, 0:TM] = dx_rows(slot, peer_rows).astype(BF16)
+            go(dx_y[slot])
+            r.xall[slot, TM:] = dx_rows(slot, my_rows).astype(BF16)
+
+        def dx_sum(slot):
+            dx_y[slot].wait_recv()
+            total = r.xall[slot, TM:].astype(F32) + r.dxy[slot].astype(F32)
+            if slot == 2:
+                dx_z[3].wait_recv()
+                total = total + r.dxz[0].astype(F32)
+            r.xall[slot, TM:] = total.astype(BF16)
+            go(dx_z[slot])
+
+        set_bias(3)
+        run(lambda p: pull(3, p))
+        dx_part(3)
+        early_finish(0)
+        set_bias(1)
+        run(lambda p: pull(1, p), {1: together((early_finish, (1,)))})
+        dx_part(1)
+        unit_s.forward(1)
+        set_bias(2)
+        run(lambda p: pull(2, p), {0: together((dx_sum, (3,))), 1: together((early_finish, (2,)))})
+        dx_part(2)
+        unit_s.forward(2)
+        set_bias(0)
+        run(lambda p: pull(0, p), {0: together((early_finish, (3,))), 1: together((dx_sum, (1,)))})
+        r.dq[...] = (acc[...].reshape(W, T).T * scale).astype(BF16)
+
+        unit_a = Unit(r.ua, r.us_r0, r.ua_out, orders[2], (r.ua_r0, r.ua_r1, r.ua_r2, r.ua_r3))
+        unit_b = Unit(r.ub, r.wo, r.ub_out, orders[3], (r.ub_r0, r.ub_r1, r.ub_r2, r.ub_r3))
+
+        def key_value_tiles(which):
+            rows = half_rows(which)
+            r.ub[rows, :] = nn(r.xt[rows, :], dkv[...]).astype(BF16)
+
+        def query_output_tiles(which):
+            rows = half_rows(which)
+            r.ua[rows, 0:W] = nn(r.xt[rows, 0:T], r.dq[...]).astype(BF16)
+            cols = pl.ds(pl.multiple_of(half_of(which) * W, 128), W)
+            r.ua[rows, W:] = tn(r.att[...], r.gm[:, cols]).astype(BF16)
+
+        key_value_tiles(0)
+        unit_b.send(0)
+        query_output_tiles(0)
+        unit_a.send(0)
+        unit_e.forward(1)
+        key_value_tiles(1)
+        unit_b.forward(0)
+        query_output_tiles(1)
+        unit_a.forward(0)
+        r.xall[0, 0:TM] = (dx_rows(0, peer_rows) + nt(r.dq[peer_rows, :], r.wqkv[:, :W])).astype(BF16)
+        go(dx_y[0])
+        r.gmix[...] += dx_rows(0, my_rows) + nt(r.dq[my_rows, :], r.wqkv[:, :W])
+        late = r.ls
+        late[0, 0:1, :] = column_sum(r.dq[...].astype(F32))
+        late[0, 1:2, :] = column_sum(dkv[:, W:].astype(F32))
+        late[0, 2:8, :] = jnp.zeros((6, W), F32)
+        late_start, late_finish = all_sum(late, r.ls_r, (CORE, XS, Z1, Z2))
+        late_start(0)
+        early_finish(4)
+        unit_s.turn()
+        late_finish(0)
+        dx_sum(2)
+        unit_s.back(3)
+        unit_e.forward(2)
+        late_finish(1)
+        unit_b.forward(1)
+        unit_s.back(2)
+        unit_a.forward(1)
+        late_finish(2)
+        unit_e.turn()
+        unit_s.back(1)
+        dx_y[0].wait_recv()
+        dx_z[1].wait_recv()
+        dx_z[2].wait_recv()
+        total = r.gmix[...] + r.dxy[0].astype(F32)
+        r.igm[...] = (total + (r.dxz[1].astype(F32) + r.dxz[2].astype(F32))).astype(BF16)
+        ig_local = local(r.igm, r.ig_out.at[my_rows])
+        ig_local.start()
+        ig_send = remote(r.igm, r.ig_out.at[my_rows], y_peer)
+        go(ig_send)
+        go(oy_send)
+        unit_b.forward(2)
+        unit_a.forward(2)
+        late_finish(3)
+        unit_e.back(3)
+        unit_b.turn()
+        unit_a.turn()
+        unit_e.back(2)
+        unit_b.back(3)
+        unit_a.back(3)
+        unit_e.back(1)
+        unit_b.back(2)
+        unit_a.back(2)
+        unit_b.back(1)
+        unit_a.back(1)
+        for unit in (unit_s, unit_e, unit_b, unit_a):
+            unit.store()
+        r.small_out[...] = r.es[1]
+        r.late_out[...] = late[0]
+        oy_local.wait()
+        oy_send.wait_recv()
+        ig_local.wait()
+        ig_send.wait_recv()
+        for unit in (unit_s, unit_e, unit_b, unit_a):
+            unit.kept.wait()
+        for p in range(HP):
+            att_copy(p).wait_send()
+        wait_sends()
+
+    return kernel
+
+
+def layer_call(sh, args):
+    T, TM, D, W, F = sh.tokens, sh.mine, sh.width, sh.hw, sh.units
+    HP = sh.pairs
+    any_spec = pl.BlockSpec(memory_space=pl.ANY)
+    vmem_spec = pl.BlockSpec(memory_space=pltpu.VMEM)
+    orders = ((CORE, XS, Z1, Z2),) * 4
+    ins = dict(
+        seg_in=vmem_spec, qb_in=vmem_spec, vb_in=vmem_spec, ob_in=vmem_spec, ag_in=vmem_spec,
+        as_in=vmem_spec, eb_in=vmem_spec, sb_in=vmem_spec, fg_in=vmem_spec, fs_in=vmem_spec,
+        x_in=any_spec, wq_in=any_spec, wk_in=any_spec, wv_in=any_spec,
+        wo_in=any_spec, we_in=any_spec, ws_in=any_spec, cot_in=any_spec,
+    )
+    outs = dict(
+        out=((T, D), BF16, any_spec),
+        ig_out=((T, D), BF16, any_spec),
+        ue_out=((D, F), BF16, any_spec),
+        us_out=((F, D), BF16, any_spec),
+        ua_out=((D, 2 * W), BF16, any_spec),
+        ub_out=((D, 2 * W), BF16, any_spec),
+        small_out=((8, D), F32, vmem_spec),
+        late_out=((8, W), F32, vmem_spec),
+    )
+    vm = lambda shape, kind: pltpu.VMEM(shape, kind)
+    scratch = dict(
+        send=pltpu.SemaphoreType.DMA((128,)),
+        recv=pltpu.SemaphoreType.DMA((128,)),
+        local=pltpu.SemaphoreType.DMA((24,)),
+        xall=vm((4, T, D), BF16),
+        xt=vm((D, 4 * T), BF16),
+        wqkv=vm((D, 3 * W), BF16),
+        wo=vm((2 * W, D), BF16),
+        we=vm((2, D, F), BF16),
+        ws=vm((2, F, D), BF16),
+        eb=vm((2, 1, F), F32),
+        cot=vm((TM, D), BF16),
+        segs=vm((4, 1, T), F32),
+        bias=vm((T, T), F32),
+        kv=vm((4, HP, 2, T, 128), BF16),
+        qm=vm((2 * HP, T, 128), BF16),
+        dm=vm((2 * HP, T, 128), BF16),
+        m_s=vm((2 * HP, 1, T), F32),
+        l_s=vm((2 * HP, 1, T), F32),
+        delta=vm((2 * HP, 1, T), F32),
+        acc=vm((2 * HP, 64, T), F32),
+        att=vm((T, W), BF16),
+        att_o=vm((TM, W), BF16),
+        n1=vm((TM, D), F32),
+        r1=vm((TM, 128), F32),
+        sec=vm((TM, D), F32),
+        gf=vm((TM, D), F32),
+        gmix=vm((TM, D), F32),
+        fl=vm((T, D), BF16),
+        flt=vm((D, T), BF16),
+        gs=vm((T, D), BF16),
+        gm=vm((T, D), BF16),
+        gp=vm((2, TM, F), F32),
+        hid=vm((T, F), BF16),
+        gpre=vm((T, F), BF16),
+        oy=vm((TM, D), BF16),
+        small=vm((8, D), F32),
+        es=vm((2, 8, D), F32),
+        es_r=vm((5, 8, D), F32),
+        ls=vm((2, 8, W), F32),
+        ls_r=vm((4, 8, W), F32),
+        dkv=vm((4 * T, 2 * W), BF16),
+        dq=vm((T, W), BF16),
+        dxy=vm((4, TM, D), BF16),
+        dxz=vm((3, TM, D), BF16),
+        igm=vm((TM, D), BF16),
+        ua=vm((D, 2 * W), BF16),
+        ub=vm((D, 2 * W), BF16),
+    )
+    for name, rows, cols in (("us", F, D), ("ue", D, F), ("ua", D, 2 * W), ("ub", D, 2 * W)):
+        for k in range(4):
+            rows = rows // 2
+            scratch[f"{name}_r{k}"] = vm((rows, cols), BF16)
+    names = list(ins) + list(outs) + list(scratch)
+    return pl.pallas_call(
+        make_kernel(sh, names, orders),
+        out_shape=[jax.ShapeDtypeStruct(o[0], o[1]) for o in outs.values()],
+        in_specs=list(ins.values()),
+        out_specs=[o[2] for o in outs.values()],
+        scratch_shapes=list(scratch.values()),
+        compiler_params=pltpu.CompilerParams(
+            collective_id=0, has_side_effects=True, vmem_limit_bytes=63 * 1024 * 1024
+        ),
+        name="layer",
+    )(*args)
+
+
+def fused_body(
+    mesh_sizes, inputs, segments, query_proj, key_proj, value_proj, query_bias, value_bias, output_proj,
+    output_bias, attn_gain, attn_shift, expand_proj, expand_bias, shrink_proj, shrink_bias,
+    final_gain, final_shift, cotangent,
+):
+    sh = Shapes(mesh_sizes, inputs.shape[0], inputs.shape[1], query_proj.shape[1], expand_proj.shape[1])
+    W = sh.hw
+    out, ig, ue, us, ua, ub, small, late = layer_call(
+        sh,
+        (
+            segments, query_bias, value_bias, output_bias, attn_gain, attn_shift, expand_bias, shrink_bias,
+            final_gain, final_shift, inputs, query_proj, key_proj, value_proj, output_proj, expand_proj,
+            shrink_proj, cotangent,
+        ),
+    )
+    ua, ub = ua.astype(F32), ub.astype(F32)
+    oproj_grad = jnp.concatenate([ua[:W, W:], ua[W:, W:]], axis=1)
+    return (
+        out, ig.astype(F32), ua[:, :W], ub[:, :W], ub[:, W:], late[0], late[1], oproj_grad,
+        small[5], small[3], small[4], ue.astype(F32), small[6:8].reshape(-1), us.astype(F32),
+        small[2], small[0], small[1],
+    )
+
+
 contract_rows = (((0,), (0,)), ((), ()))
 contract_cols = (((1,), (1,)), ((), ()))
 
@@ -290,4 +1117,7 @@
         P(),
         P(),
     )
-    return jax.shard_map(body, mesh=mesh, in_specs=in_specs, out_specs=out_specs, check_vma=False)
+    sizes = dict(mesh.shape)
+    fits = sizes == {"dp": 4, "ctx": 4, "tensor": 2}
+    chosen = functools.partial(fused_body, sizes) if fits else body
+    return jax.shard_map(chosen, mesh=mesh, in_specs=in_specs, out_specs=out_specs, check_vma=False)

time: 746 us -> 243 us (0.33)
  waiting for transfers between devices: 438 us -> 0 us
  Pallas kernels: 0 us -> 226 us
  matrix products: 141 us -> 0 us
  blocking collectives: 74.9 us -> 0 us
  local copies, waits for them, and re-layouts: 44.8 us -> 7.62 us
  other arithmetic: 29.9 us -> 7.73 us
  between operations: 14.4 us -> 0.7 us
    psum x5 -> x0, waiting for transfers between devices: 329 us -> none  [the longest x1 232 us: body(): lax.psum((query_grad, key_grad, value_grad, qbias_grad, vbias_grad, oproj...]
    pallas_call x0 -> x1, Pallas kernels: none -> 226 us  [layer_call(): pl.pallas_call(make_kernel(sh, names, orders), out_shape=[jax.ShapeDtypeS...]
    dot_general x60 -> x0, matrix products: 141 us -> none  [the longest x24 52.3 us: inner_cols(): lax.dot_general(left, right, contract_cols, preferred_element_type=jnp.fl...]
    psum x1 -> x0, blocking collectives: 61.2 us -> none  [body(): lax.psum((query_grad, key_grad, value_grad, qbias_grad, vbias_grad, oproj...]
    reduce_scatter x2 -> x0, waiting for transfers between devices: 55.5 us -> none  [the longest x1 33.8 us: body(): lax.psum_scatter(join_heads(value_back).astype(jnp.bfloat16), 'ctx', scat...]
    all_gather x2 -> x0, waiting for transfers between devices: 52.4 us -> none  [the longest x1 31.5 us: body(): lax.all_gather(values, 'ctx', axis=0, tiled=True)]
    unnamed x122 -> x15, local copies, waits for them, and re-layouts: 29.6 us -> 1.2 us
    reduce_sum x15 -> x0, other arithmetic: 18.5 us -> none  [the longest x6 7.47 us: head_forward(): row_sum = jnp.sum(exp_scores, axis=1, keepdims=True)]
  transfers between devices with their start and end apart: 9 -> 0, of which waited for: 8 -> 0; matrix products, arithmetic and copies ran while one was open for 5% -> 0% of each run, Pallas kernels for 0% -> 0%
where the time goes in v1:
time: 243 us; the launch traced here: 242 us
  Pallas kernels  226 us (93%)
  other arithmetic  7.73 us (3%)
  local copies, waits for them, and re-layouts  7.62 us (3%)
    pallas_call x1, Pallas kernels, layer_call(): pl.pallas_call(make_kernel(sh, names, orders), out_shape=[jax.ShapeDtypeS...  226 us

profile of v1, /device:TPU:0, one launch (start us, length us, event | category | flops | bytes accessed | tf_op | source)
XLA Modules:
  0.0 242.1 jit_solution(14553433267916614471)
XLA Ops:
  0.7 226.1 %layer.1 = (bf16[512,768]{1,0:T(8,128)(2,1)}, bf16[512,768]{1,0:T(8,128)(2,1)}, bf16[768,1536]{1,0:T(8,128)(2,1)}, bf16[1536,768]{1,0:T(8,128)(2,1)}, bf16[768,7...) custom-call(s32[1,512]{1,0:T(1,128)} %refs_0_.1, bf16[384]{0:T(512)(128)(2,1)} %refs_1_.1, ...), custom_call_target="tpu_custom_call" | custom-call | tf_op jit(solution)/shard_map/layer/pallas_call | solution.py:801
  226.8 1.1 fusion
  227.9 0.0 copy-start.6
  227.9 0.0 copy-start.1
  227.9 1.1 pad_maximum_fusion
  229.0 0.0 copy-done.6
  229.0 0.6 slice_reduce_fusion
  229.7 0.0 copy-done.1
  229.7 0.0 copy-start
  229.7 1.6 fusion.1
  231.2 0.2 copy-done
  231.4 0.0 copy-start.3
  231.4 1.1 slice.56
  232.5 0.6 reshape.37
  233.1 1.4 slice_reduce_fusion.6
  234.5 0.0 copy-done.3
  234.5 0.0 copy-start.2
  234.5 2.8 %convert_element_type.18 = f32[768,1536]{1,0:T(8,128)} convert(bf16[768,1536]{1,0:T(8,128)(2,1)S(1)} %copy-done.3) | non-fusion elementwise | flops 1179648 | bytes 7077888 | tf_op jit(solution)/shard_map/convert_element_type | solution.py:833
  237.3 0.0 copy-done.2
  237.3 2.5 %convert_element_type.19 = f32[1536,768]{1,0:T(8,128)} convert(bf16[1536,768]{1,0:T(8,128)(2,1)S(1)} %copy-done.2) | non-fusion elementwise | flops 1179648 | bytes 7077888 | tf_op jit(solution)/shard_map/convert_element_type | solution.py:833
  239.9 0.0 copy-done.5
  239.9 1.3 convert_element_type.15
  241.1 0.1 copy-done.4
  241.3 0.9 copy.36
  (3 shorter events, 0.0 us)
Async XLA Ops:
  227.9 1.1 copy-start.6
  227.9 1.8 copy-start.1
  229.7 1.7 copy-start
  231.4 3.1 %copy-start.3 = (bf16[768,1536]{1,0:T(8,128)(2,1)S(1)}, bf16[768,1536]{1,0:T(8,128)(2,1)}, u32[]{:S(2)}) copy-start(bf16[768,1536]{1,0:T(8,128)(2,1)} %get-tuple-element.31) | copy-start | bytes 7077892
  234.5 2.8 %copy-start.2 = (bf16[1536,768]{1,0:T(8,128)(2,1)S(1)}, bf16[1536,768]{1,0:T(8,128)(2,1)}, u32[]{:S(2)}) copy-start(bf16[1536,768]{1,0:T(8,128)(2,1)} %get-tuple-element.32) | copy-start | bytes 7077892
  237.3 2.5 %copy-start.5 = (bf16[512,768]{1,0:T(8,128)(2,1)S(1)}, bf16[512,768]{1,0:T(8,128)(2,1)}, u32[]{:S(2)}) copy-start(bf16[512,768]{1,0:T(8,128)(2,1)} %get-tuple-element.26) | copy-start | bytes 2359300
  239.9 1.4 copy-start.4

commit v2 on v1

--- a/solution.py
+++ b/solution.py
@@ -97,10 +97,11 @@
             assert counts[kind] <= (send_ref, local_ref)[kind].shape[0], counts
             return at
 
-        def remote(src, dst, device, at=None):
+        def remote(src, dst, device, at=None, recv_at=None):
             at = take(0) if at is None else at
+            recv_at = at if recv_at is None else recv_at
             return pltpu.make_async_remote_copy(
-                src_ref=src, dst_ref=dst, send_sem=send_ref.at[at], recv_sem=recv_ref.at[at],
+                src_ref=src, dst_ref=dst, send_sem=send_ref.at[at], recv_sem=recv_ref.at[recv_at],
                 device_id=device, device_id_type=MESH,
             )
 
@@ -109,15 +110,23 @@
 
         unsent = []
 
-        def go(copy):
-            copy.start()
-            unsent.append(copy)
+        def go(copy, where=None):
+            if where is None:
+                copy.start()
+            else:
+                pl.when(where)(lambda: copy.start())
+            unsent.append((copy, where))
 
         def wait_sends(*but):
-            for copy in unsent:
-                if not any(copy is other for other in but):
+            kept = [entry for entry in unsent if any(entry[0] is other for other in but)]
+            for copy, where in unsent:
+                if any(copy is other for other in but):
+                    continue
+                if where is None:
                     copy.wait_send()
-            unsent[:] = but
+                else:
+                    pl.when(where)(lambda copy=copy: copy.wait_send())
+            unsent[:] = kept
 
         loads = types.SimpleNamespace(
             x=local(r.x_in, r.xall.at[0]),
@@ -149,31 +158,49 @@
         ]
         eb_copy = remote(r.eb.at[0], r.eb.at[1], y_peer)
         x_rows = [pl.ds(pl.multiple_of(t * TM + k * PR, PR), PR) for k in range(PARTS)]
-        x_z, x_y = {}, {}
+        mid = lax.rem(low_bit + high_bit, 2)
+        is_mid = mid == 1
+        slots = (0, 1, 2 + mid, 3 - mid)
+        x_at = take(0, 3 * PARTS)
+
+        def x_recv(slot, k):
+            return x_at + (slot - 1) * PARTS + k
+
+        def x_move(src_slot, dst_slot, peer, k):
+            src = r.x_in.at[x_rows[k]] if src_slot == 0 else r.xall.at[src_slot, x_rows[k]]
+            return remote(src, r.xall.at[dst_slot, x_rows[k]], peer, None, x_recv(dst_slot, k))
+
+        x_near = [x_move(0, 1, z1_peer, k) for k in range(PARTS)]
+        x_far = [x_move(0, 3, z3_peer, k) for k in range(PARTS)]
+        x_next = (
+            None,
+            [x_move(1, 2, z3_peer, k) for k in range(PARTS)],
+            [x_move(3, 2, z1_peer, k) for k in range(PARTS)],
+            [x_move(2, 3, z1_peer, k) for k in range(PARTS)],
+        )
+        x_y = [None] + [
+            [remote(r.xall.at[slots[o], x_rows[k]], r.xall.at[slots[o], x_rows[k]], y_peer) for k in range(PARTS)]
+            for o in (1, 2, 3)
+        ]
         for k in range(PARTS):
-            mine = x_rows[k]
-            x_z[1, k] = remote(r.x_in.at[mine], r.xall.at[1, mine], z1_peer)
-            x_z[2, k] = remote(r.x_in.at[mine], r.xall.at[2, mine], z2_peer)
-            x_z[3, k] = remote(r.xall.at[2, mine], r.xall.at[3, mine], z1_peer)
-            for slot in (1, 2, 3):
-                x_y[slot, k] = remote(r.xall.at[slot, mine], r.xall.at[slot, mine], y_peer)
-        for slot in (1, 2):
-            for k in range(PARTS):
-                go(x_z[slot, k])
+            go(x_near[k])
+            go(x_far[k], is_mid)
         for copy in seg_copies[1:]:
             go(copy)
         go(eb_copy)
 
-        def pass_on(slot, k):
-            x_z[slot, k].wait_recv()
-            go(x_y[slot, k])
-            if slot == 2:
-                go(x_z[3, k])
-
-        def block_here(slot):
-            seg_copies[slot].wait_recv()
+        def arrive(o, k):
+            here = r.xall.at[slots[o], x_rows[k]]
+            remote(here, here, z1_peer, x_at, x_recv(slots[o], k)).wait_recv()
+            go(x_next[o][k], is_mid)
+            go(x_y[o][k])
+
+        def block_here(o):
+            if o == 1:
+                for copy in seg_copies[1:]:
+                    copy.wait_recv()
             for k in range(PARTS):
-                x_y[slot, k].wait_recv()
+                x_y[o][k].wait_recv()
 
         chunks = [
             (r.wo_in, r.wo.at[pl.ds(W, W)], W, 0, 1),
@@ -226,7 +253,7 @@
             for copy in w_core[i]:
                 copy.wait_recv()
 
-        for i in range(2):
+        for i in range(3):
             go(w_y[i])
 
         kv = r.kv
@@ -296,34 +323,40 @@
             return all_of
 
         set_bias(0)
-        run(lambda p: attend(0, p), {0: together((pass_on, (1, 0))), 2: together((pass_on, (1, 1)))})
+
+        def flip_inputs(slot):
+            at = slot * T if isinstance(slot, int) else pl.multiple_of(slot * T, T)
+            r.xt[:, pl.ds(at, T)] = r.xall[slot].T
+
+        def next_block(o):
+            block_here(o)
+            set_keys_values(slots[o])
+            set_bias(slots[o])
+
         hop1(0)
-        go(w_y[2])
-        for slot in (1, 2, 3):
-            if slot == 1:
-                r.xt[:, 0:T] = r.xall[0].T
-                block_here(1)
-                set_keys_values(1)
-                set_bias(1)
-                run(lambda p: attend(1, p), {0: together((pass_on, (2, 0))), 2: together((hop2, (0,)), (hop1, (1,)))})
-                pass_on(2, 1)
-                go(w_y[3])
-                r.xt[:, T : 2 * T] = r.xall[1].T
-            elif slot == 2:
-                block_here(2)
-                set_keys_values(2)
-                set_bias(2)
-                run(lambda p: attend(2, p), {0: together((hop2, (1,)), (hop3, (0,))), 2: together((pass_on, (3, 0)))})
-                hop1(2)
-                go(w_y[4])
-                r.xt[:, 2 * T : 3 * T] = r.xall[2].T
-                pass_on(3, 1)
-                hop3(1)
-                hop2(2)
-            else:
-                block_here(3)
-                set_keys_values(3)
-                set_bias(3)
+        run(lambda p: attend(0, p), {1: together((arrive, (1, 0))), 2: together((hop1, (1,)))})
+        arrive(1, 1)
+        go(w_y[3])
+        hop1(2)
+        flip_inputs(0)
+        hop2(0)
+        arrive(2, 0)
+        hop2(1)
+        hop3(0)
+        arrive(2, 1)
+        go(w_y[4])
+        next_block(1)
+        run(lambda p: attend(1, p), {0: together((hop3, (1,))), 2: together((hop2, (2,)), (hop1, (3,)))})
+        arrive(3, 0)
+        hop3(2)
+        flip_inputs(1)
+        arrive(3, 1)
+        next_block(2)
+        run(lambda p: attend(slots[2], p), {0: together((hop2, (3,))), 2: together((hop1, (4,)))})
+        hop3(3)
+        flip_inputs(slots[2])
+        hop2(4)
+        next_block(3)
         att_at = take(0, HP)
 
         def att_copy(p):
@@ -331,24 +364,19 @@
             return remote(r.att.at[peer_rows, cols], r.att_o.at[:, cols], y_peer, att_at + p)
 
         for p in range(HP):
-            attend(3, p)
+            attend(slots[3], p)
             for h in (2 * p, 2 * p + 1):
                 acc[h] = acc[h] / l_s[h]
                 m_s[h] = m_s[h] + jnp.log(l_s[h])
             pair = acc[2 * p : 2 * p + 2].reshape(128, T).T
             r.att[:, p * 128 : (p + 1) * 128] = pair.astype(BF16)
             att_copy(p).start()
-            if p == 0:
-                hop1(3)
-            if p == 1:
-                hop3(2)
-        hop2(3)
         loads.wo.wait()
         weights_done(0)
         loads.cot.wait()
 
         mix = nn(r.att[my_rows, :], r.wo[0:W, :])
-        r.xt[:, 3 * T :] = r.xall[3].T
+        flip_inputs(slots[3])
         for p in range(HP):
             att_copy(p).wait_recv()
         mix = mix + nn(r.att_o[...], r.wo[W : 2 * W, :])
@@ -361,7 +389,7 @@
         fl_copy = remote(r.fl.at[my_rows], r.fl.at[my_rows], y_peer)
         loads.we.wait()
         loads.ws.wait()
-        hop1(4)
+        hop3(4)
         go(fl_copy)
 
 
@@ -386,14 +414,9 @@
             lax.fori_loop(0, NTILE, step, 0)
 
         tiles(lambda j: forward_tile(0, j))
-        hop3(3)
-        hop2(4)
         eb_copy.wait_recv()
-        weights_done(1)
-        weights_done(2)
-        hop3(4)
-        weights_done(3)
-        weights_done(4)
+        for i in range(1, len(chunks)):
+            weights_done(i)
         tiles(lambda j: forward_tile(1, j))
         normed2, recip2 = normalise(r.sec[...])
         upstream = r.cot[...].astype(F32)
@@ -436,17 +459,25 @@
 
         class Unit:
             def __init__(self, grad, whole, out, order, bufs):
-                self.grad, self.whole, self.out, self.order, self.bufs = grad, whole, out, order, bufs
+                self.grad, self.order, self.bufs = grad, order, bufs
                 self.first, self.rows = [0], [grad.shape[0]]
                 for stage in order:
                     self.rows.append(self.rows[-1] // 2)
                     self.first.append(self.first[-1] + bit_of[stage] * self.rows[-1])
-                self.down, self.up = {}, {}
+                self.down, self.up = [], []
+                for k, stage in enumerate(order):
+                    rows = self.rows[k + 1]
+                    theirs = rows_at(grad, self.first[k] + (1 - bit_of[stage]) * rows, rows)
+                    self.down.append(remote(theirs, bufs[k], peer_of[stage]))
+                    target = rows_at(whole, self.first[k + 1], rows)
+                    source = target
+                    if k == len(order) - 1:
+                        source = rows_at(grad, self.first[k + 1], rows)
+                        self.kept = local(source, target)
+                    self.up.append(remote(source, target, peer_of[stage]))
+                self.stored = local(whole, out)
 
             def send(self, k):
-                stage, rows = self.order[k], self.rows[k + 1]
-                theirs = self.first[k] + (1 - bit_of[stage]) * rows
-                self.down[k] = remote(rows_at(self.grad, theirs, rows), self.bufs[k], peer_of[stage])
                 go(self.down[k])
 
             def add(self, k):
@@ -467,14 +498,8 @@
                 self.send(k + 1)
 
             def spread(self, k):
-                rows, first_row = self.rows[k + 1], self.first[k + 1]
-                target = rows_at(self.whole, first_row, rows)
-                last = k == len(self.order) - 1
-                source = rows_at(self.grad, first_row, rows) if last else target
-                self.up[k] = remote(source, target, peer_of[self.order[k]])
                 go(self.up[k])
-                if last:
-                    self.kept = local(source, target)
+                if k == len(self.order) - 1:
                     self.kept.start()
 
             def turn(self):
@@ -490,8 +515,7 @@
 
             def store(self):
                 self.up[0].wait_recv()
-                self.kept = local(self.whole, self.out)
-                self.kept.start()
+                self.stored.start()
 
         def all_sum(buf, slots, stages):
             copies = [remote(buf.at[k % 2], slots.at[k], peer_of[stage]) for k, stage in enumerate(stages)]
@@ -525,6 +549,9 @@
         wait_sends(gm_copy)
         unit_s = Unit(r.ws.at[1], r.ws.at[0], r.us_out, orders[0], (r.us_r0, r.us_r1, r.us_r2, r.us_r3))
         unit_e = Unit(r.we.at[1], r.we.at[0], r.ue_out, orders[1], (r.ue_r0, r.ue_r1, r.ue_r2, r.ue_r3))
+
+        unit_a = Unit(r.ua, r.us_r0, r.ua_out, orders[2], (r.ua_r0, r.ua_r1, r.ua_r2, r.ua_r3))
+        unit_b = Unit(r.ub, r.wo, r.ub_out, orders[3], (r.ub_r0, r.ub_r1, r.ub_r2, r.ub_r3))
 
         def half_of(which):
             return which * core + (1 - which) * (1 - core)
@@ -625,19 +652,18 @@
         dx_part(3)
         early_finish(0)
         set_bias(1)
-        run(lambda p: pull(1, p), {1: together((early_finish, (1,)))})
+        run(lambda p: pull(1, p), {1: together((unit_s.forward, (1,)))})
+        early_finish(1)
         dx_part(1)
-        unit_s.forward(1)
         set_bias(2)
-        run(lambda p: pull(2, p), {0: together((dx_sum, (3,))), 1: together((early_finish, (2,)))})
+        run(lambda p: pull(2, p), {2: together((unit_s.forward, (2,)), (dx_sum, (3,)))})
         dx_part(2)
-        unit_s.forward(2)
         set_bias(0)
-        run(lambda p: pull(0, p), {0: together((early_finish, (3,))), 1: together((dx_sum, (1,)))})
+        run(lambda p: pull(0, p), {1: together((unit_s.turn, ()), (unit_e.forward, (1,)))})
         r.dq[...] = (acc[...].reshape(W, T).T * scale).astype(BF16)
-
-        unit_a = Unit(r.ua, r.us_r0, r.ua_out, orders[2], (r.ua_r0, r.ua_r1, r.ua_r2, r.ua_r3))
-        unit_b = Unit(r.ub, r.wo, r.ub_out, orders[3], (r.ub_r0, r.ub_r1, r.ub_r2, r.ub_r3))
+        unit_s.back(3)
+        early_finish(2)
+
 
         def key_value_tiles(which):
             rows = half_rows(which)
@@ -653,9 +679,9 @@
         unit_b.send(0)
         query_output_tiles(0)
         unit_a.send(0)
-        unit_e.forward(1)
         key_value_tiles(1)
         unit_b.forward(0)
+        unit_e.forward(2)
         query_output_tiles(1)
         unit_a.forward(0)
         r.xall[0, 0:TM] = (dx_rows(0, peer_rows) + nt(r.dq[peer_rows, :], r.wqkv[:, :W])).astype(BF16)
@@ -667,19 +693,26 @@
         late[0, 2:8, :] = jnp.zeros((6, W), F32)
         late_start, late_finish = all_sum(late, r.ls_r, (CORE, XS, Z1, Z2))
         late_start(0)
+        unit_s.back(2)
+        early_finish(3)
+        late_finish(0)
+        unit_e.turn()
+        dx_sum(1)
+        dx_sum(2)
+        unit_b.forward(1)
+        unit_e.back(3)
+        unit_a.forward(1)
         early_finish(4)
-        unit_s.turn()
-        late_finish(0)
-        dx_sum(2)
-        unit_s.back(3)
-        unit_e.forward(2)
+        unit_b.forward(2)
+        unit_e.back(2)
+        unit_b.turn()
+        unit_a.forward(2)
+        unit_b.back(3)
+        unit_a.turn()
+        unit_b.back(2)
+        unit_a.back(3)
+        unit_a.back(2)
         late_finish(1)
-        unit_b.forward(1)
-        unit_s.back(2)
-        unit_a.forward(1)
-        late_finish(2)
-        unit_e.turn()
-        unit_s.back(1)
         dx_y[0].wait_recv()
         dx_z[1].wait_recv()
         dx_z[2].wait_recv()
@@ -690,22 +723,16 @@
         ig_send = remote(r.igm, r.ig_out.at[my_rows], y_peer)
         go(ig_send)
         go(oy_send)
-        unit_b.forward(2)
-        unit_a.forward(2)
+        late_finish(2)
+        unit_s.back(1)
         late_finish(3)
-        unit_e.back(3)
-        unit_b.turn()
-        unit_a.turn()
-        unit_e.back(2)
-        unit_b.back(3)
-        unit_a.back(3)
         unit_e.back(1)
-        unit_b.back(2)
-        unit_a.back(2)
+        unit_s.store()
         unit_b.back(1)
+        unit_e.store()
         unit_a.back(1)
-        for unit in (unit_s, unit_e, unit_b, unit_a):
-            unit.store()
+        unit_b.store()
+        unit_a.store()
         r.small_out[...] = r.es[1]
         r.late_out[...] = late[0]
         oy_local.wait()
@@ -713,7 +740,7 @@
         ig_local.wait()
         ig_send.wait_recv()
         for unit in (unit_s, unit_e, unit_b, unit_a):
-            unit.kept.wait()
+            unit.stored.wait()
         for p in range(HP):
             att_copy(p).wait_send()
         wait_sends()
@@ -811,14 +838,112 @@
     )(*args)
 
 
+def finish_kernel(sh, names, *refs):
+    r = types.SimpleNamespace(**dict(zip(names, refs)))
+    W = sh.hw
+    half = sh.units // 2
+    pieces = []
+    for at in range(2):
+        pieces.append((r.us.at[pl.ds(at * half, half)], r.us_v.at[at], r.usf.at[at], r.us_out.at[pl.ds(at * half, half)]))
+    for at in range(2):
+        rows = pl.ds(at * W, W)
+        pieces.append((r.ue.at[rows], r.ue_v.at[at], r.uef.at[at], r.ue_out.at[rows]))
+    cols = [pl.ds(0, W), pl.ds(W, W)]
+    pieces.append((r.ub.at[:, cols[0]], r.ab_v.at[0], r.abf.at[0], r.wk_out))
+    pieces.append((r.ub.at[:, cols[1]], r.ab_v.at[1], r.abf.at[1], r.wv_out))
+    pieces.append((r.ua.at[:, cols[0]], r.ab_v.at[2], r.abf.at[2], r.wq_out))
+    for at in range(2):
+        rows = pl.ds(at * W, W)
+        pieces.append((r.ua.at[rows, cols[1]], r.o_v.at[at], r.of.at[at], r.wo_out.at[:, cols[at]]))
+    pieces.append((r.ig, r.ig_v, r.igf, r.ig_out))
+    passed = pltpu.make_async_copy(r.out, r.out_out, r.sems.at[0])
+    passed.start()
+    reads = [pltpu.make_async_copy(p[0], p[1], r.sems.at[1 + k]) for k, p in enumerate(pieces)]
+    for copy in reads:
+        copy.start()
+    small = r.small[...]
+    for name, at in (("fg", 0), ("fs", 1), ("sb", 2), ("ag", 3), ("as_", 4), ("ob", 5)):
+        getattr(r, name)[...] = small[at]
+    r.eb[0 : sh.width] = small[6]
+    r.eb[sh.width :] = small[7]
+    r.qb[...] = r.late[0]
+    r.vb[...] = r.late[1]
+    writes = []
+    for k, (_, low, wide, target) in enumerate(pieces):
+        reads[k].wait()
+        rows = low.shape[0]
+        step = 96 if rows % 96 == 0 else 64
+
+        def tile(i, carry):
+            at = pl.ds(pl.multiple_of(i * step, step), step)
+            wide[at, :] = low[at, :].astype(F32)
+            return carry
+
+        lax.fori_loop(0, rows // step, tile, 0)
+        copy = pltpu.make_async_copy(wide, target, r.sems.at[1 + len(pieces) + k])
+        copy.start()
+        writes.append(copy)
+    passed.wait()
+    for copy in writes:
+        copy.wait()
+
+
+def finish_call(sh, parts):
+    T, D, W, F = sh.tokens, sh.width, sh.hw, sh.units
+    any_spec = pl.BlockSpec(memory_space=pl.ANY)
+    hbm_spec = pl.BlockSpec(memory_space=pltpu.HBM)
+    vmem_spec = pl.BlockSpec(memory_space=pltpu.VMEM)
+    ins = dict(
+        out=hbm_spec, ig=hbm_spec, ue=hbm_spec, us=hbm_spec, ua=hbm_spec, ub=hbm_spec,
+        small=vmem_spec, late=vmem_spec,
+    )
+    outs = dict(
+        out_out=((T, D), BF16, any_spec),
+        ig_out=((T, D), F32, any_spec),
+        wq_out=((D, W), F32, any_spec),
+        wk_out=((D, W), F32, any_spec),
+        wv_out=((D, W), F32, any_spec),
+        qb=((W,), F32, vmem_spec),
+        vb=((W,), F32, vmem_spec),
+        wo_out=((W, D), F32, any_spec),
+        ob=((D,), F32, vmem_spec),
+        ag=((D,), F32, vmem_spec),
+        as_=((D,), F32, vmem_spec),
+        ue_out=((D, F), F32, any_spec),
+        eb=((F,), F32, vmem_spec),
+        us_out=((F, D), F32, any_spec),
+        sb=((D,), F32, vmem_spec),
+        fg=((D,), F32, vmem_spec),
+        fs=((D,), F32, vmem_spec),
+    )
+    scratch = dict(sems=pltpu.SemaphoreType.DMA((24,)))
+    for low, wide, shape in (
+        ("us_v", "usf", (2, F // 2, D)),
+        ("ue_v", "uef", (2, W, F)),
+        ("ab_v", "abf", (3, D, W)),
+        ("o_v", "of", (2, W, W)),
+        ("ig_v", "igf", (T, D)),
+    ):
+        scratch[low], scratch[wide] = pltpu.VMEM(shape, BF16), pltpu.VMEM(shape, F32)
+    names = list(ins) + list(outs) + list(scratch)
+    return pl.pallas_call(
+        functools.partial(finish_kernel, sh, names),
+        out_shape=[jax.ShapeDtypeStruct(o[0], o[1]) for o in outs.values()],
+        in_specs=list(ins.values()),
+        out_specs=[o[2] for o in outs.values()],
+        scratch_shapes=list(scratch.values()),
+        compiler_params=pltpu.CompilerParams(vmem_limit_bytes=63 * 1024 * 1024),
+        name="finish",
+    )(*parts)
+
+
 def fused_body(
     mesh_sizes, inputs, segments, query_proj, key_proj, value_proj, query_bias, value_bias, output_proj,
     output_bias, attn_gain, attn_shift, expand_proj, expand_bias, shrink_proj, shrink_bias,
     final_gain, final_shift, cotangent,
 ):
     sh = Shapes(mesh_sizes, inputs.shape[0], inputs.shape[1], query_proj.shape[1], expand_proj.shape[1])
-    W = sh.hw
-    out, ig, ue, us, ua, ub, small, late = layer_call(
+    parts = layer_call(
         sh,
         (
             segments, query_bias, value_bias, output_bias, attn_gain, attn_shift, expand_bias, shrink_bias,
@@ -826,13 +951,7 @@
             shrink_proj, cotangent,
         ),
     )
-    ua, ub = ua.astype(F32), ub.astype(F32)
-    oproj_grad = jnp.concatenate([ua[:W, W:], ua[W:, W:]], axis=1)
-    return (
-        out, ig.astype(F32), ua[:, :W], ub[:, :W], ub[:, W:], late[0], late[1], oproj_grad,
-        small[5], small[3], small[4], ue.astype(F32), small[6:8].reshape(-1), us.astype(F32),
-        small[2], small[0], small[1],
-    )
+    return finish_call(sh, parts)
 
 
 contract_rows = (((0,), (0,)), ((), ()))

time: 243 us -> 240 us (0.988)
  Pallas kernels: 226 us -> 239 us
  other arithmetic: 7.73 us -> 0 us
  local copies, waits for them, and re-layouts: 7.62 us -> 0 us
    pallas_call x0 -> x1, Pallas kernels: none -> 26.5 us  [finish_call(): pl.pallas_call(functools.partial(finish_kernel, sh, names), out_shape=[ja...]
    pallas_call x1, Pallas kernels: 226 us -> 213 us  [layer_call(): pl.pallas_call(make_kernel(sh, names, orders), out_shape=[jax.ShapeDtypeS...]
    convert_element_type x3 -> x0, other arithmetic: 6.63 us -> none  [the longest x1 2.83 us: fused_body(): ue.astype(F32)]
    slice x6 -> x0, local copies, waits for them, and re-layouts: 5.8 us -> none  [the longest x1 1.55 us: fused_body(): ub[:, W:]]
where the time goes in v2:
time: 240 us
  Pallas kernels  239 us (100%)
    pallas_call x1, Pallas kernels, layer_call(): pl.pallas_call(make_kernel(sh, names, orders), out_shape=[jax.ShapeDtypeS...  213 us
    pallas_call x1, Pallas kernels, finish_call(): pl.pallas_call(functools.partial(finish_kernel, sh, names), out_shape=[ja...  26.5 us

profile of v2, /device:TPU:0, one launch (start us, length us, event | category | flops | bytes accessed | tf_op | source)
XLA Modules:
  0.0 240.1 jit_solution(15550363978837007269)
XLA Ops:
  0.7 212.7 %layer.1 = (bf16[512,768]{1,0:T(8,128)(2,1)}, bf16[512,768]{1,0:T(8,128)(2,1)}, bf16[768,1536]{1,0:T(8,128)(2,1)}, bf16[1536,768]{1,0:T(8,128)(2,1)}, bf16[768,7...) custom-call(s32[1,512]{1,0:T(1,128)} %refs_0_.1, bf16[384]{0:T(512)(128)(2,1)} %refs_1_.1, ...), custom_call_target="tpu_custom_call" | custom-call | tf_op jit(solution)/shard_map/layer/pallas_call | solution.py:828
  213.4 26.5 %finish.1 = (bf16[512,768]{1,0:T(8,128)(2,1)}, f32[512,768]{1,0:T(8,128)}, f32[768,384]{1,0:T(8,128)}, f32[768,384]{1,0:T(8,128)}, f32[768,384]{1,0:T(8,128)}, /...) custom-call(bf16[512,768]{1,0:T(8,128)(2,1)} %get-tuple-element.25.r, ...), custom_call_target="tpu_custom_call" | custom-call | tf_op jit(solution)/shard_map/finish/pallas_call | solution.py:929

commit v3 on v2

--- a/solution.py
+++ b/solution.py
@@ -12,7 +12,7 @@
 norm_eps = 1e-12
 masked = -1e30
 MESH = pl.DeviceIdType.MESH
-CORE, XS, YS, Z1, Z2 = range(5)
+CORE, XS, YS, Z1, Z2, LINE = range(6)
 BF16, F32 = jnp.bfloat16, jnp.float32
 INV_SQRT2 = 0.7071067811865476
 INV_SQRT_2PI = 0.3989422804014327
@@ -64,7 +64,7 @@
         self.pairs = heads_width // 128
 
 
-def make_kernel(sh, names, orders):
+def make_kernel(sh, names):
     T, TM, D, W, F = sh.tokens, sh.mine, sh.width, sh.hw, sh.units
     HP = sh.pairs
     TILE = 512
@@ -159,7 +159,7 @@
         eb_copy = remote(r.eb.at[0], r.eb.at[1], y_peer)
         x_rows = [pl.ds(pl.multiple_of(t * TM + k * PR, PR), PR) for k in range(PARTS)]
         mid = lax.rem(low_bit + high_bit, 2)
-        is_mid = mid == 1
+        is_mid, is_end = mid == 1, mid == 0
         slots = (0, 1, 2 + mid, 3 - mid)
         x_at = take(0, 3 * PARTS)
 
@@ -460,38 +460,60 @@
         class Unit:
             def __init__(self, grad, whole, out, order, bufs):
                 self.grad, self.order, self.bufs = grad, order, bufs
-                self.first, self.rows = [0], [grad.shape[0]]
+                self.first, self.rows, self.line = [0], [grad.shape[0]], None
                 for stage in order:
-                    self.rows.append(self.rows[-1] // 2)
-                    self.first.append(self.first[-1] + bit_of[stage] * self.rows[-1])
+                    self.rows.append(self.rows[-1] // (4 if stage == LINE else 2))
+                    at = c if stage == LINE else bit_of[stage]
+                    self.first.append(self.first[-1] + at * self.rows[-1])
                 self.down, self.up = [], []
                 for k, stage in enumerate(order):
-                    rows = self.rows[k + 1]
+                    rows, last = self.rows[k + 1], k == len(order) - 1
+                    target = rows_at(whole, self.first[k + 1], rows)
+                    source = target
+                    if last:
+                        source = rows_at(grad, self.first[k + 1], rows)
+                        self.kept = local(source, target)
+                    if stage == LINE:
+                        self.line = k
+                        self.far = self.first[k] + 2 * (1 - high_bit) * rows
+                        self.edge = self.first[k] + 3 * high_bit * rows
+                        near = self.first[k] + 2 * high_bit * rows
+                        ends = grad.at[pl.ds(pl.multiple_of(self.first[k] + (1 - high_bit) * rows, rows), 3 * rows)]
+                        self.down.append(
+                            (
+                                remote(ends, bufs[k][0], z1_peer),
+                                remote(rows_at(grad, self.far, 2 * rows), bufs[k][1], z3_peer),
+                                remote(rows_at(grad, self.edge, rows), bufs[k][2], z1_peer),
+                            )
+                        )
+                        near, far = rows_at(whole, near, 2 * rows), rows_at(whole, self.far, 2 * rows)
+                        self.up.append(
+                            (remote(source, target, z1_peer), remote(near, near, z3_peer), remote(far, far, z1_peer))
+                        )
+                        continue
                     theirs = rows_at(grad, self.first[k] + (1 - bit_of[stage]) * rows, rows)
                     self.down.append(remote(theirs, bufs[k], peer_of[stage]))
-                    target = rows_at(whole, self.first[k + 1], rows)
-                    source = target
-                    if k == len(order) - 1:
-                        source = rows_at(grad, self.first[k + 1], rows)
-                        self.kept = local(source, target)
                     self.up.append(remote(source, target, peer_of[stage]))
                 self.stored = local(whole, out)
 
+            def add_rows(self, first_row, rows, terms, step):
+
+                def tile(i, carry):
+                    window = self.grad.at[pl.ds(pl.multiple_of(first_row + i * step, step), step)]
+                    total = window[...].astype(F32)
+                    for buf, at in terms:
+                        total = total + buf[pl.ds(pl.multiple_of(at + i * step, step), step), :].astype(F32)
+                    window[...] = total.astype(BF16)
+                    return carry
+
+                lax.fori_loop(0, rows // step, tile, 0)
+
             def send(self, k):
                 go(self.down[k])
 
             def add(self, k):
                 self.down[k].wait_recv()
-                rows, first_row = self.rows[k + 1], self.first[k + 1]
-                step = next(v for v in (96, 48) if rows % v == 0)
-
-                def tile(i, carry):
-                    window = self.grad.at[pl.ds(pl.multiple_of(first_row + i * step, step), step)]
-                    there = pl.ds(pl.multiple_of(i * step, step), step)
-                    window[...] = (window[...].astype(F32) + self.bufs[k][there, :].astype(F32)).astype(BF16)
-                    return carry
-
-                lax.fori_loop(0, rows // step, tile, 0)
+                self.add_rows(self.first[k + 1], self.rows[k + 1], [(self.bufs[k], 0)], min(96, self.rows[k + 1]))
 
             def forward(self, k):
                 self.add(k)
@@ -502,16 +524,93 @@
                 if k == len(self.order) - 1:
                     self.kept.start()
 
+            def back(self, k):
+                if k == len(self.order) - 1:
+                    self.kept.wait()
+                self.up[k].wait_recv()
+                if self.line is not None and k - 1 == self.line:
+                    go(self.up[k - 1][0])
+                else:
+                    self.spread(k - 1)
+
+            def za(self):
+                go(self.down[self.line][0], is_end)
+
+            def zb(self):
+                k = self.line
+                rows = self.rows[k + 1]
+
+                @pl.when(is_mid)
+                def _():
+                    self.down[k][0].wait_recv()
+                    self.add_rows(self.far, 2 * rows, [(self.bufs[k][0], (1 - high_bit) * rows)], rows)
+
+                go(self.down[k][1], is_mid)
+
+            def zc(self):
+                k = self.line
+                rows, (first_buf, second_buf, _) = self.rows[k + 1], self.bufs[k]
+
+                @pl.when(is_mid)
+                def _():
+                    self.down[k][1].wait_recv()
+                    self.add_rows(self.edge, rows, [(second_buf, high_bit * rows)], rows)
+
+                go(self.down[k][2], is_mid)
+
+                @pl.when(is_mid)
+                def _():
+                    terms = [(first_buf, 2 * high_bit * rows), (second_buf, (1 - high_bit) * rows)]
+                    self.add_rows(self.first[k + 1], rows, terms, rows)
+                    if k == len(self.order) - 1:
+                        self.kept.start()
+                        self.up[k][0].start()
+
+            def zd(self):
+                k = self.line
+
+                @pl.when(is_end)
+                def _():
+                    self.down[k][2].wait_recv()
+                    self.add_rows(self.first[k + 1], self.rows[k + 1], [(self.bufs[k][2], 0)], self.rows[k + 1])
+                    if k == len(self.order) - 1:
+                        self.kept.start()
+                        self.up[k][0].start()
+
+                if k == len(self.order) - 1:
+                    unsent.append((self.up[k][0], None))
+
+            def ze(self):
+                k = self.line
+
+                @pl.when(is_mid)
+                def _():
+                    if k == len(self.order) - 1:
+                        self.kept.wait()
+                    self.up[k][0].wait_recv()
+
+                go(self.up[k][1], is_mid)
+
+            def zf(self):
+                pl.when(is_mid)(lambda: self.up[self.line][1].wait_recv())
+                go(self.up[self.line][2], is_mid)
+
+            def zg(self):
+                k = self.line
+
+                @pl.when(is_end)
+                def _():
+                    if k == len(self.order) - 1:
+                        self.kept.wait()
+                    self.up[k][0].wait_recv()
+                    self.up[k][2].wait_recv()
+
+                self.spread(k - 1)
+
             def turn(self):
                 k = len(self.order) - 1
                 self.add(k)
                 self.spread(k)
-
-            def back(self, k):
-                if k == len(self.order) - 1:
-                    self.kept.wait()
-                self.up[k].wait_recv()
-                self.spread(k - 1)
 
             def store(self):
                 self.up[0].wait_recv()
@@ -547,24 +646,39 @@
 
         tiles(other_tile)
         wait_sends(gm_copy)
-        unit_s = Unit(r.ws.at[1], r.ws.at[0], r.us_out, orders[0], (r.us_r0, r.us_r1, r.us_r2, r.us_r3))
-        unit_e = Unit(r.we.at[1], r.we.at[0], r.ue_out, orders[1], (r.ue_r0, r.ue_r1, r.ue_r2, r.ue_r3))
-
-        unit_a = Unit(r.ua, r.us_r0, r.ua_out, orders[2], (r.ua_r0, r.ua_r1, r.ua_r2, r.ua_r3))
-        unit_b = Unit(r.ub, r.wo, r.ub_out, orders[3], (r.ub_r0, r.ub_r1, r.ub_r2, r.ub_r3))
+        by_line, by_pairs = (CORE, XS, LINE), (CORE, XS, Z1, Z2)
+        half_d = D // 2
+
+        def line_unit(grad, whole, out, first_buf, k):
+            steps = (r.l0.at[k], r.l1.at[k], r.l2.at[k])
+            return Unit(grad, whole, out, by_line, (first_buf, r.x0.at[k], steps))
+
+        def pair_unit(grad, whole, out, k):
+            return Unit(grad, whole, out, by_pairs, (r.p0.at[k], r.p1.at[k], r.p2.at[k], r.p3.at[k]))
+
+        s1, s2 = [
+            line_unit(r.ws.at[1, pl.ds(at, D)], r.ws.at[0, pl.ds(at, D)], r.us_out.at[pl.ds(at, D)], first_buf, k)
+            for k, (at, first_buf) in enumerate(((0, r.s0.at[pl.ds(0, half_d)]), (D, r.s0.at[pl.ds(half_d, half_d)])))
+        ]
+        e1, e2 = [
+            line_unit(
+                r.we.at[1, :, pl.ds(at, D)], r.we.at[0, :, pl.ds(at, D)], r.ue_out.at[:, pl.ds(at, D)], r.e0.at[k - 2], k
+            )
+            for k, at in ((2, 0), (3, D))
+        ]
+        ua = pair_unit(r.ua, r.s0, r.ua_out, 0)
+        ub = pair_unit(r.ub, r.wo, r.ub_out, 1)
 
         def half_of(which):
             return which * core + (1 - which) * (1 - core)
 
         def shrink_tiles(which):
-            base = half_of(which) * (F // 2)
-
             def tile(i, carry):
-                at = pl.multiple_of(base + i * 384, 128)
-                r.ws[1, pl.ds(at, 384), :] = tn(r.hid[:, pl.ds(at, 384)], r.gs[...]).astype(BF16)
+                at = pl.multiple_of(i * D + half_of(which) * half_d, 128)
+                r.ws[1, pl.ds(at, half_d), :] = tn(r.hid[:, pl.ds(at, half_d)], r.gs[...]).astype(BF16)
                 return carry
 
-            lax.fori_loop(0, F // 2 // 384, tile, 0)
+            lax.fori_loop(0, F // D, tile, 0)
 
         def half_rows(which):
             return pl.ds(pl.multiple_of(half_of(which) * (D // 2), D // 2), D // 2)
@@ -578,29 +692,24 @@
 
             tiles(tile)
 
-        shrink_tiles(0)
-        unit_s.send(0)
-        r.flt[...] = r.fl[...].T
-        shrink_tiles(1)
-        expand_tiles(0)
-        unit_e.send(0)
-        unit_s.forward(0)
-        expand_tiles(1)
-        unit_e.forward(0)
-        totals = column_sum(r.gpre[...].astype(F32))
-        small[6:7, :] = totals[:, :D]
-        small[7:8, :] = totals[:, D:]
-        r.es[0] = small[...]
+        def sum_blocks():
+            totals = column_sum(r.gpre[...].astype(F32))
+            small[6:7, :] = totals[:, :D]
+            small[7:8, :] = totals[:, D:]
+            r.es[0] = small[...]
+
         early_start, early_finish = all_sum(r.es, r.es_r, (YS, CORE, XS, Z1, Z2))
-        early_start(0)
-
-        gm_copy.wait_recv()
-        grad_att = nt(r.gm[...], r.wo[0:W, :]).astype(BF16).astype(F32)
-        flipped = grad_att.T.reshape(2 * HP, 64, T)
-        r.delta[...] = jnp.sum(acc[...] * flipped, axis=1, keepdims=True)
-        for p in range(HP):
-            split_pair(r.dm, p, grad_att[:, p * 128 : (p + 1) * 128])
-        acc[...] = jnp.zeros_like(acc)
+        late_start, late_finish = all_sum(r.ls, r.ls_r, (CORE, XS, Z1, Z2))
+
+        def grad_heads():
+            gm_copy.wait_recv()
+            grad_att = nt(r.gm[...], r.wo[0:W, :]).astype(BF16).astype(F32)
+            flipped = grad_att.T.reshape(2 * HP, 64, T)
+            r.delta[...] = jnp.sum(acc[...] * flipped, axis=1, keepdims=True)
+            for p in range(HP):
+                split_pair(r.dm, p, grad_att[:, p * 128 : (p + 1) * 128])
+            acc[...] = jnp.zeros_like(acc)
+
         oy_send = remote(r.oy, r.out.at[my_rows], y_peer)
         dkv = r.dkv
 
@@ -623,11 +732,12 @@
             dkv[rows, pl.ds(pl.multiple_of(W + p * 128, 128), 128)] = grad_v.astype(BF16)
 
         dx_y = [remote(r.xall.at[k, pl.ds(0, TM)], r.dxy.at[k], y_peer) for k in range(SLOTS)]
-        dx_z = {
-            3: remote(r.xall.at[3, pl.ds(TM, TM)], r.dxz.at[0], z1_peer),
-            1: remote(r.xall.at[1, pl.ds(TM, TM)], r.dxz.at[1], z1_peer),
-            2: remote(r.xall.at[2, pl.ds(TM, TM)], r.dxz.at[2], z2_peer),
-        }
+
+        def dx_move(slot, target, peer):
+            return remote(r.xall.at[slot, pl.ds(TM, TM)], r.dxz.at[target], peer)
+
+        dx_end = {3: dx_move(3, 0, z1_peer), 2: dx_move(2, 1, z1_peer), 1: dx_move(1, 2, z1_peer)}
+        dx_mid = {3: dx_move(3, 3, z3_peer), 2: dx_move(2, 4, z3_peer), 1: dx_move(1, 5, z1_peer)}
 
         def dx_rows(slot, rows):
             here = pl.ds(pl.multiple_of(slot * T + rows.start, TM), TM)
@@ -641,28 +751,37 @@
         def dx_sum(slot):
             dx_y[slot].wait_recv()
             total = r.xall[slot, TM:].astype(F32) + r.dxy[slot].astype(F32)
-            if slot == 2:
-                dx_z[3].wait_recv()
-                total = total + r.dxz[0].astype(F32)
             r.xall[slot, TM:] = total.astype(BF16)
-            go(dx_z[slot])
-
-        set_bias(3)
-        run(lambda p: pull(3, p))
-        dx_part(3)
-        early_finish(0)
-        set_bias(1)
-        run(lambda p: pull(1, p), {1: together((unit_s.forward, (1,)))})
-        early_finish(1)
-        dx_part(1)
-        set_bias(2)
-        run(lambda p: pull(2, p), {2: together((unit_s.forward, (2,)), (dx_sum, (3,)))})
-        dx_part(2)
-        set_bias(0)
-        run(lambda p: pull(0, p), {1: together((unit_s.turn, ()), (unit_e.forward, (1,)))})
-        r.dq[...] = (acc[...].reshape(W, T).T * scale).astype(BF16)
-        unit_s.back(3)
-        early_finish(2)
+            go(dx_end[slot], is_end)
+
+        def dx_pass(slot):
+            came = {3: dx_end[2], 2: dx_end[3], 1: dx_mid[2]}[slot]
+            at = {3: 1, 2: 0, 1: 4}[slot]
+
+            @pl.when(is_mid)
+            def _():
+                came.wait_recv()
+                total = r.xall[slot, TM:].astype(F32) + r.dxz[at].astype(F32)
+                r.xall[slot, TM:] = total.astype(BF16)
+
+            go(dx_mid[slot], is_mid)
+
+        def dx_last():
+            dx_y[0].wait_recv()
+            r.gmix[...] += r.dxy[0].astype(F32)
+
+            @pl.when(is_mid)
+            def _():
+                dx_end[1].wait_recv()
+                dx_mid[3].wait_recv()
+                r.gmix[...] += r.dxz[2].astype(F32) + r.dxz[3].astype(F32)
+
+            @pl.when(is_end)
+            def _():
+                dx_mid[1].wait_recv()
+                r.gmix[...] += r.dxz[5].astype(F32)
+
+            r.igm[...] = r.gmix[...].astype(BF16)
 
 
         def key_value_tiles(which):
@@ -675,71 +794,156 @@
             cols = pl.ds(pl.multiple_of(half_of(which) * W, 128), W)
             r.ua[rows, W:] = tn(r.att[...], r.gm[:, cols]).astype(BF16)
 
+        def query_grads():
+            r.dq[...] = (acc[...].reshape(W, T).T * scale).astype(BF16)
+            r.ls[0, 0:1, :] = column_sum(r.dq[...].astype(F32))
+            r.ls[0, 1:2, :] = column_sum(dkv[:, W:].astype(F32))
+            r.ls[0, 2:8, :] = jnp.zeros((6, W), F32)
+
+        def dx_own():
+            r.xall[0, 0:TM] = (dx_rows(0, peer_rows) + nt(r.dq[peer_rows, :], r.wqkv[:, :W])).astype(BF16)
+            go(dx_y[0])
+            r.gmix[...] += dx_rows(0, my_rows) + nt(r.dq[my_rows, :], r.wqkv[:, :W])
+
+        ig_local = local(r.igm, r.ig_out.at[my_rows])
+        ig_send = remote(r.igm, r.ig_out.at[my_rows], y_peer)
+
+        def dx_out():
+            dx_last()
+            ig_local.start()
+            go(ig_send)
+
+        shrink_tiles(0)
+        s1.send(0)
+        s2.send(0)
+        r.flt[...] = r.fl[...].T
+        shrink_tiles(1)
+        expand_tiles(0)
+        e1.send(0)
+        e2.send(0)
+        go(oy_send)
+        s1.forward(0)
+        expand_tiles(1)
+        sum_blocks()
+        early_start(0)
+        grad_heads()
+        set_bias(3)
+
+        def beside_30():
+            e2.forward(0)
+
+        run(lambda p: pull(3, p), {0: beside_30})
+        s1.add(1)
+        s1.za()
+        dx_part(3)
+        early_finish(0)
+        e1.forward(0)
+        set_bias(2)
+
+        def beside_21():
+            s1.zb()
+
+        run(lambda p: pull(2, p), {1: beside_21})
+        e2.add(1)
+        e2.za()
+        dx_part(2)
+        early_finish(1)
+        s2.forward(0)
+        set_bias(1)
+
+        def beside_10():
+            s1.zc()
+
+
+        def beside_11():
+            e2.zb()
+            e1.add(1)
+            e1.za()
+
+        run(lambda p: pull(1, p), {0: beside_10, 1: beside_11})
+        s1.zd()
+        dx_part(1)
+        set_bias(0)
+
+        def beside_00():
+            e2.zc()
+            e1.zb()
+            s2.add(1)
+            s2.za()
+
+        run(lambda p: pull(0, p), {0: beside_00})
+        e2.zd()
+        query_grads()
+        late_start(0)
         key_value_tiles(0)
-        unit_b.send(0)
+        ub.send(0)
+        late_finish(0)
+        s1.ze()
+        dx_sum(3)
+        e1.zc()
         query_output_tiles(0)
-        unit_a.send(0)
+        ua.send(0)
         key_value_tiles(1)
-        unit_b.forward(0)
-        unit_e.forward(2)
+        ub.forward(0)
+        s2.zb()
+        s1.zf()
         query_output_tiles(1)
-        unit_a.forward(0)
-        r.xall[0, 0:TM] = (dx_rows(0, peer_rows) + nt(r.dq[peer_rows, :], r.wqkv[:, :W])).astype(BF16)
-        go(dx_y[0])
-        r.gmix[...] += dx_rows(0, my_rows) + nt(r.dq[my_rows, :], r.wqkv[:, :W])
-        late = r.ls
-        late[0, 0:1, :] = column_sum(r.dq[...].astype(F32))
-        late[0, 1:2, :] = column_sum(dkv[:, W:].astype(F32))
-        late[0, 2:8, :] = jnp.zeros((6, W), F32)
-        late_start, late_finish = all_sum(late, r.ls_r, (CORE, XS, Z1, Z2))
-        late_start(0)
-        unit_s.back(2)
+        early_finish(2)
+        ua.forward(0)
+        e1.zd()
+        e2.ze()
+        s2.zc()
+        ub.forward(1)
+        s2.zd()
+        e1.ze()
+        s1.zg()
         early_finish(3)
-        late_finish(0)
-        unit_e.turn()
+        late_finish(1)
+        ub.forward(2)
+        s2.ze()
+        e1.zf()
+        ua.forward(1)
+        ub.turn()
+        e1.zg()
+        early_finish(4)
+        ua.forward(2)
+        ub.back(3)
+        ua.turn()
+        dx_sum(2)
+        s2.zf()
+        dx_pass(2)
+        e1.back(1)
+        e2.zf()
+        dx_own()
+        ub.back(2)
+        late_finish(2)
+        ua.back(3)
         dx_sum(1)
-        dx_sum(2)
-        unit_b.forward(1)
-        unit_e.back(3)
-        unit_a.forward(1)
-        early_finish(4)
-        unit_b.forward(2)
-        unit_e.back(2)
-        unit_b.turn()
-        unit_a.forward(2)
-        unit_b.back(3)
-        unit_a.turn()
-        unit_b.back(2)
-        unit_a.back(3)
-        unit_a.back(2)
-        late_finish(1)
-        dx_y[0].wait_recv()
-        dx_z[1].wait_recv()
-        dx_z[2].wait_recv()
-        total = r.gmix[...] + r.dxy[0].astype(F32)
-        r.igm[...] = (total + (r.dxz[1].astype(F32) + r.dxz[2].astype(F32))).astype(BF16)
-        ig_local = local(r.igm, r.ig_out.at[my_rows])
-        ig_local.start()
-        ig_send = remote(r.igm, r.ig_out.at[my_rows], y_peer)
-        go(ig_send)
-        go(oy_send)
-        late_finish(2)
-        unit_s.back(1)
+        s1.back(1)
+        s2.zg()
         late_finish(3)
-        unit_e.back(1)
-        unit_s.store()
-        unit_b.back(1)
-        unit_e.store()
-        unit_a.back(1)
-        unit_b.store()
-        unit_a.store()
+        dx_pass(3)
+        ub.back(1)
+        dx_pass(1)
+        e2.zg()
+        s2.back(1)
+        s2.store()
+        ua.back(2)
+        dx_out()
+        s1.store()
+        e2.back(1)
+        ua.back(1)
+        e1.store()
+        ua.store()
+        e2.store()
+        ub.store()
         r.small_out[...] = r.es[1]
-        r.late_out[...] = late[0]
+        r.late_out[...] = r.ls[0]
         oy_local.wait()
         oy_send.wait_recv()
         ig_local.wait()
         ig_send.wait_recv()
-        for unit in (unit_s, unit_e, unit_b, unit_a):
+        for unit in (s1, s2, e1, e2, ua, ub):
             unit.stored.wait()
         for p in range(HP):
             att_copy(p).wait_send()
@@ -753,7 +957,6 @@
     HP = sh.pairs
     any_spec = pl.BlockSpec(memory_space=pl.ANY)
     vmem_spec = pl.BlockSpec(memory_space=pltpu.VMEM)
-    orders = ((CORE, XS, Z1, Z2),) * 4
     ins = dict(
         seg_in=vmem_spec, qb_in=vmem_spec, vb_in=vmem_spec, ob_in=vmem_spec, ag_in=vmem_spec,
         as_in=vmem_spec, eb_in=vmem_spec, sb_in=vmem_spec, fg_in=vmem_spec, fs_in=vmem_spec,
@@ -772,8 +975,8 @@
     )
     vm = lambda shape, kind: pltpu.VMEM(shape, kind)
     scratch = dict(
-        send=pltpu.SemaphoreType.DMA((128,)),
-        recv=pltpu.SemaphoreType.DMA((128,)),
+        send=pltpu.SemaphoreType.DMA((160,)),
+        recv=pltpu.SemaphoreType.DMA((160,)),
         local=pltpu.SemaphoreType.DMA((24,)),
         xall=vm((4, T, D), BF16),
         xt=vm((D, 4 * T), BF16),
@@ -815,18 +1018,24 @@
         dkv=vm((4 * T, 2 * W), BF16),
         dq=vm((T, W), BF16),
         dxy=vm((4, TM, D), BF16),
-        dxz=vm((3, TM, D), BF16),
+        dxz=vm((6, TM, D), BF16),
         igm=vm((TM, D), BF16),
         ua=vm((D, 2 * W), BF16),
         ub=vm((D, 2 * W), BF16),
-    )
-    for name, rows, cols in (("us", F, D), ("ue", D, F), ("ua", D, 2 * W), ("ub", D, 2 * W)):
-        for k in range(4):
-            rows = rows // 2
-            scratch[f"{name}_r{k}"] = vm((rows, cols), BF16)
+        s0=vm((D, D), BF16),
+        e0=vm((2, D // 2, D), BF16),
+        x0=vm((4, D // 4, D), BF16),
+        l0=vm((4, 3 * (D // 16), D), BF16),
+        l1=vm((4, 2 * (D // 16), D), BF16),
+        l2=vm((4, D // 16, D), BF16),
+        p0=vm((2, D // 2, D), BF16),
+        p1=vm((2, D // 4, D), BF16),
+        p2=vm((2, D // 8, D), BF16),
+        p3=vm((2, D // 16, D), BF16),
+    )
     names = list(ins) + list(outs) + list(scratch)
     return pl.pallas_call(
-        make_kernel(sh, names, orders),
+        make_kernel(sh, names),
         out_shape=[jax.ShapeDtypeStruct(o[0], o[1]) for o in outs.values()],
         in_specs=list(ins.values()),
         out_specs=[o[2] for o in outs.values()],
@@ -856,11 +1065,14 @@
         rows = pl.ds(at * W, W)
         pieces.append((r.ua.at[rows, cols[1]], r.o_v.at[at], r.of.at[at], r.wo_out.at[:, cols[at]]))
     pieces.append((r.ig, r.ig_v, r.igf, r.ig_out))
-    passed = pltpu.make_async_copy(r.out, r.out_out, r.sems.at[0])
-    passed.start()
+    taken = pltpu.make_async_copy(r.out, r.out_v, r.sems.at[0])
+    taken.start()
     reads = [pltpu.make_async_copy(p[0], p[1], r.sems.at[1 + k]) for k, p in enumerate(pieces)]
     for copy in reads:
         copy.start()
+    taken.wait()
+    passed = pltpu.make_async_copy(r.out_v, r.out_out, r.sems.at[2 * len(pieces) + 1])
+    passed.start()
     small = r.small[...]
     for name, at in (("fg", 0), ("fs", 1), ("sb", 2), ("ag", 3), ("as_", 4), ("ob", 5)):
         getattr(r, name)[...] = small[at]
@@ -916,7 +1128,7 @@
         fg=((D,), F32, vmem_spec),
         fs=((D,), F32, vmem_spec),
     )
-    scratch = dict(sems=pltpu.SemaphoreType.DMA((24,)))
+    scratch = dict(sems=pltpu.SemaphoreType.DMA((24,)), out_v=pltpu.VMEM((T, D), BF16))
     for low, wide, shape in (
         ("us_v", "usf", (2, F // 2, D)),
         ("ue_v", "uef", (2, W, F)),

time: 240 us -> 195 us (0.81)
  Pallas kernels: 239 us -> 194 us
    pallas_call x1, Pallas kernels: 213 us -> 184 us  [layer_call(): pl.pallas_call(make_kernel(sh, names), out_shape=[jax.ShapeDtypeStruct(o[...]
    pallas_call x1, Pallas kernels: 26.5 us -> 9.52 us  [finish_call(): pl.pallas_call(functools.partial(finish_kernel, sh, names), out_shape=[ja...]
where the time goes in v3:
time: 195 us
  Pallas kernels  194 us (99%)
    pallas_call x1, Pallas kernels, layer_call(): pl.pallas_call(make_kernel(sh, names), out_shape=[jax.ShapeDtypeStruct(o[...  184 us
    pallas_call x1, Pallas kernels, finish_call(): pl.pallas_call(functools.partial(finish_kernel, sh, names), out_shape=[ja...  9.52 us

profile of v3, /device:TPU:0, one launch (start us, length us, event | category | flops | bytes accessed | tf_op | source)
XLA Modules:
  0.0 194.7 jit_solution(7696656335399830168)
XLA Ops:
  0.7 184.4 %layer.1 = (bf16[512,768]{1,0:T(8,128)(2,1)}, bf16[512,768]{1,0:T(8,128)(2,1)}, bf16[768,1536]{1,0:T(8,128)(2,1)}, bf16[1536,768]{1,0:T(8,128)(2,1)}, bf16[768,7...) custom-call(s32[1,512]{1,0:T(1,128)} %refs_0_.1, bf16[384]{0:T(512)(128)(2,1)} %refs_1_.1, ...), custom_call_target="tpu_custom_call" | custom-call | tf_op jit(solution)/shard_map/layer/pallas_call | solution.py:1037
  185.0 9.5 %finish.1 = (bf16[512,768]{1,0:T(8,128)(2,1)}, f32[512,768]{1,0:T(8,128)}, f32[768,384]{1,0:T(8,128)}, f32[768,384]{1,0:T(8,128)}, f32[768,384]{1,0:T(8,128)}, /...) custom-call(bf16[512,768]{1,0:T(8,128)(2,1)} %get-tuple-element.25.r, ...), custom_call_target="tpu_custom_call" | custom-call | tf_op jit(solution)/shard_map/finish/pallas_call | solution.py:1141

commit v4 on v3

--- a/solution.py
+++ b/solution.py
@@ -253,10 +253,8 @@
             for copy in w_core[i]:
                 copy.wait_recv()
 
-        for i in range(3):
-            go(w_y[i])
-
-        kv = r.kv
+
+        kv, m_s, l_s, acc = r.kv, r.m_s, r.l_s, r.acc
         value_bias = row(r.vb_in)
         scale = HEAD_DIM ** (-0.5)
         lane = lax.broadcasted_iota(jnp.int32, (T, 128), 1)
@@ -278,19 +276,20 @@
                 cols = slice(j * 128, (j + 1) * 128)
                 r.bias[:, cols] = jnp.where(seg_keys == r.segs[0, :, cols], 0.0, masked)
 
-        loads.x.wait()
-        loads.wk.wait()
-        loads.wv.wait()
-        set_keys_values(0)
-        loads.wq.wait()
-        queries = (nn(r.xall[0], r.wqkv[:, :W]) + row(r.qb_in)).astype(BF16).astype(F32) * scale
-        for p in range(HP):
-            split_pair(r.qm, p, queries[:, p * 128 : (p + 1) * 128])
-
-        m_s, l_s, acc = r.m_s, r.l_s, r.acc
-        m_s[...] = jnp.full_like(m_s, masked)
-        l_s[...] = jnp.zeros_like(l_s)
-        acc[...] = jnp.zeros_like(acc)
+        def project():
+            loads.x.wait()
+            loads.wk.wait()
+            loads.wv.wait()
+            set_keys_values(0)
+            loads.wq.wait()
+            queries = (nn(r.xall[0], r.wqkv[:, :W]) + row(r.qb_in)).astype(BF16).astype(F32) * scale
+            for p in range(HP):
+                split_pair(r.qm, p, queries[:, p * 128 : (p + 1) * 128])
+            m_s[...] = jnp.full_like(m_s, masked)
+            l_s[...] = jnp.zeros_like(l_s)
+            acc[...] = jnp.zeros_like(acc)
+            set_bias(0)
+
 
         def attend(slot, p):
             pair_keys = kv[slot, p, 0]
@@ -322,8 +321,6 @@
 
             return all_of
 
-        set_bias(0)
-
         def flip_inputs(slot):
             at = slot * T if isinstance(slot, int) else pl.multiple_of(slot * T, T)
             r.xt[:, pl.ds(at, T)] = r.xall[slot].T
@@ -333,37 +330,13 @@
             set_keys_values(slots[o])
             set_bias(slots[o])
 
-        hop1(0)
-        run(lambda p: attend(0, p), {1: together((arrive, (1, 0))), 2: together((hop1, (1,)))})
-        arrive(1, 1)
-        go(w_y[3])
-        hop1(2)
-        flip_inputs(0)
-        hop2(0)
-        arrive(2, 0)
-        hop2(1)
-        hop3(0)
-        arrive(2, 1)
-        go(w_y[4])
-        next_block(1)
-        run(lambda p: attend(1, p), {0: together((hop3, (1,))), 2: together((hop2, (2,)), (hop1, (3,)))})
-        arrive(3, 0)
-        hop3(2)
-        flip_inputs(1)
-        arrive(3, 1)
-        next_block(2)
-        run(lambda p: attend(slots[2], p), {0: together((hop2, (3,))), 2: together((hop1, (4,)))})
-        hop3(3)
-        flip_inputs(slots[2])
-        hop2(4)
-        next_block(3)
         att_at = take(0, HP)
 
         def att_copy(p):
             cols = pl.ds(p * 128, 128)
             return remote(r.att.at[peer_rows, cols], r.att_o.at[:, cols], y_peer, att_at + p)
 
-        for p in range(HP):
+        def attend_last(p):
             attend(slots[3], p)
             for h in (2 * p, 2 * p + 1):
                 acc[h] = acc[h] / l_s[h]
@@ -371,27 +344,24 @@
             pair = acc[2 * p : 2 * p + 2].reshape(128, T).T
             r.att[:, p * 128 : (p + 1) * 128] = pair.astype(BF16)
             att_copy(p).start()
-        loads.wo.wait()
-        weights_done(0)
-        loads.cot.wait()
-
-        mix = nn(r.att[my_rows, :], r.wo[0:W, :])
-        flip_inputs(slots[3])
-        for p in range(HP):
-            att_copy(p).wait_recv()
-        mix = mix + nn(r.att_o[...], r.wo[W : 2 * W, :])
-        normed, recip = normalise(r.xall[0, my_rows, :].astype(F32) + mix + vec[0])
-        r.n1[...] = normed
-        r.r1[...] = jnp.broadcast_to(recip, (TM, 128))
-        first = normed * vec[1] + vec[2]
-        r.sec[...] = first + vec[3]
-        r.fl[my_rows, :] = first.astype(BF16)
+
         fl_copy = remote(r.fl.at[my_rows], r.fl.at[my_rows], y_peer)
-        loads.we.wait()
-        loads.ws.wait()
-        hop3(4)
-        go(fl_copy)
-
+
+        def out_project():
+            loads.wo.wait()
+            r.sec[...] = nn(r.att[my_rows, :], r.wo[0:W, :])
+
+        def first_norm():
+            for p in range(HP):
+                att_copy(p).wait_recv()
+            mix = r.sec[...] + nn(r.att_o[...], r.wo[W : 2 * W, :])
+            normed, recip = normalise(r.xall[0, my_rows, :].astype(F32) + mix + vec[0])
+            r.n1[...] = normed
+            r.r1[...] = jnp.broadcast_to(recip, (TM, 128))
+            first = normed * vec[1] + vec[2]
+            r.sec[...] = first + vec[3]
+            r.fl[my_rows, :] = first.astype(BF16)
+            go(fl_copy)
 
         def tile_cols(j):
             return pl.ds(pl.multiple_of(j * TILE, TILE), TILE)
@@ -413,11 +383,80 @@
 
             lax.fori_loop(0, NTILE, step, 0)
 
-        tiles(lambda j: forward_tile(0, j))
-        eb_copy.wait_recv()
-        for i in range(1, len(chunks)):
-            weights_done(i)
-        tiles(lambda j: forward_tile(1, j))
+        def own_units():
+            loads.we.wait()
+            loads.ws.wait()
+            tiles(lambda j: forward_tile(0, j))
+
+        def other_units():
+            eb_copy.wait_recv()
+            tiles(lambda j: forward_tile(1, j))
+
+        go(w_y[0])
+        go(w_y[1])
+        project()
+        arrive(1, 0)
+
+        def with_00():
+            go(w_y[2])
+            go(w_y[3])
+            hop1(0)
+            arrive(1, 1)
+            arrive(2, 0)
+            hop2(0)
+            hop1(1)
+
+
+        def with_01():
+            arrive(2, 1)
+
+        run(lambda p: attend(slots[0], p), {0: with_00, 1: with_01})
+        arrive(3, 0)
+        hop2(1)
+        next_block(1)
+
+        def with_11():
+            arrive(3, 1)
+            hop1(2)
+            go(w_y[4])
+            hop3(0)
+
+        run(lambda p: attend(slots[1], p), {1: with_11})
+        hop1(3)
+        next_block(2)
+
+        def with_20():
+            hop3(1)
+
+
+        def with_21():
+            hop2(2)
+
+        run(lambda p: attend(slots[2], p), {0: with_20, 1: with_21})
+        hop2(3)
+        weights_done(0)
+        next_block(3)
+        attend_last(0)
+        hop1(4)
+        attend_last(1)
+        attend_last(2)
+        flip_inputs(slots[1])
+        hop2(4)
+        out_project()
+        first_norm()
+        hop3(2)
+        flip_inputs(slots[2])
+        flip_inputs(slots[3])
+        weights_done(1)
+        hop3(3)
+        weights_done(2)
+        flip_inputs(slots[0])
+        hop3(4)
+        own_units()
+        weights_done(3)
+        weights_done(4)
+        other_units()
+        loads.cot.wait()
         normed2, recip2 = normalise(r.sec[...])
         upstream = r.cot[...].astype(F32)
         grad_second = denormalise(upstream * vec[4], normed2, recip2)
@@ -634,18 +673,27 @@
 
             return start, finish
 
-        fl_copy.wait_recv()
-        gs_copy.wait_recv()
-
-        def other_tile(j):
+
+        def other_hidden(j):
             cols = tile_cols(j)
             pre = nn(r.fl[peer_rows, :], r.we[0, :, cols]) + r.eb[0, :, cols]
             hidden, slope = gelu_parts(pre)
             r.hid[peer_rows, cols] = hidden.astype(BF16)
-            r.gpre[peer_rows, cols] = (nt(r.gs[peer_rows, :], r.ws[0, cols, :]) * slope).astype(BF16)
-
-        tiles(other_tile)
+            r.gp[0, :, cols] = slope
+
+        def other_slopes():
+            def tile(j):
+                cols = tile_cols(j)
+                low = nt(r.gs[peer_rows, :], r.ws[0, cols, :]) * r.gp[0, :, cols]
+                r.gpre[peer_rows, cols] = low.astype(BF16)
+
+            tiles(tile)
+
+        fl_copy.wait_recv()
+        tiles(other_hidden)
+        r.flt[...] = r.fl[...].T
         wait_sends(gm_copy)
+        gs_copy.wait_recv()
         by_line, by_pairs = (CORE, XS, LINE), (CORE, XS, Z1, Z2)
         half_d = D // 2
 
@@ -656,10 +704,13 @@
         def pair_unit(grad, whole, out, k):
             return Unit(grad, whole, out, by_pairs, (r.p0.at[k], r.p1.at[k], r.p2.at[k], r.p3.at[k]))
 
-        s1, s2 = [
-            line_unit(r.ws.at[1, pl.ds(at, D)], r.ws.at[0, pl.ds(at, D)], r.us_out.at[pl.ds(at, D)], first_buf, k)
-            for k, (at, first_buf) in enumerate(((0, r.s0.at[pl.ds(0, half_d)]), (D, r.s0.at[pl.ds(half_d, half_d)])))
-        ]
+        s1 = Unit(
+            r.ws.at[1, pl.ds(0, D)], r.ws.at[0, pl.ds(0, D)], r.us_out.at[pl.ds(0, D)], (CORE, LINE, XS),
+            (r.s0.at[pl.ds(0, half_d)], (r.z0, r.z1, r.z2), r.z3),
+        )
+        s2 = line_unit(
+            r.ws.at[1, pl.ds(D, D)], r.ws.at[0, pl.ds(D, D)], r.us_out.at[pl.ds(D, D)], r.s0.at[pl.ds(half_d, half_d)], 1
+        )
         e1, e2 = [
             line_unit(
                 r.we.at[1, :, pl.ds(at, D)], r.we.at[0, :, pl.ds(at, D)], r.ue_out.at[:, pl.ds(at, D)], r.e0.at[k - 2], k
@@ -816,133 +867,135 @@
         shrink_tiles(0)
         s1.send(0)
         s2.send(0)
-        r.flt[...] = r.fl[...].T
+        other_slopes()
         shrink_tiles(1)
         expand_tiles(0)
         e1.send(0)
         e2.send(0)
         go(oy_send)
-        s1.forward(0)
+        s1.add(0)
+        s1.za()
         expand_tiles(1)
         sum_blocks()
         early_start(0)
+        s2.forward(0)
         grad_heads()
+        e1.forward(0)
         set_bias(3)
-
-        def beside_30():
+        run(lambda p: pull(3, p))
+        set_bias(2)
+
+        def beside_20():
+            s2.add(1)
+            s2.za()
+            s1.zb()
             e2.forward(0)
 
-        run(lambda p: pull(3, p), {0: beside_30})
-        s1.add(1)
-        s1.za()
-        dx_part(3)
-        early_finish(0)
-        e1.forward(0)
-        set_bias(2)
-
-        def beside_21():
-            s1.zb()
-
-        run(lambda p: pull(2, p), {1: beside_21})
-        e2.add(1)
-        e2.za()
-        dx_part(2)
-        early_finish(1)
-        s2.forward(0)
+        run(lambda p: pull(2, p), {0: beside_20})
         set_bias(1)
 
         def beside_10():
-            s1.zc()
-
-
-        def beside_11():
-            e2.zb()
             e1.add(1)
             e1.za()
+            early_finish(0)
+            s2.zb()
+
+
+        def beside_11():
+            s1.zc()
 
         run(lambda p: pull(1, p), {0: beside_10, 1: beside_11})
-        s1.zd()
-        dx_part(1)
         set_bias(0)
 
         def beside_00():
-            e2.zc()
             e1.zb()
-            s2.add(1)
-            s2.za()
+            early_finish(1)
+            s2.zc()
+            e2.add(1)
+            e2.za()
+            dx_part(3)
+            s1.zd()
+            s1.send(2)
 
         run(lambda p: pull(0, p), {0: beside_00})
-        e2.zd()
+        s1.add(2)
+        s1.spread(2)
         query_grads()
         late_start(0)
+        e1.zc()
+        s2.zd()
+        e2.zb()
         key_value_tiles(0)
         ub.send(0)
-        late_finish(0)
-        s1.ze()
-        dx_sum(3)
-        e1.zc()
+        s1.back(2)
         query_output_tiles(0)
         ua.send(0)
+        s2.ze()
+        e1.zd()
         key_value_tiles(1)
         ub.forward(0)
-        s2.zb()
+        dx_sum(3)
+        e2.zc()
+        s1.ze()
+        e2.zd()
+        late_finish(0)
+        dx_part(2)
+        s2.zf()
+        query_output_tiles(1)
+        ub.forward(1)
+        early_finish(2)
+        e1.ze()
+        s2.zg()
+        ua.forward(0)
         s1.zf()
-        query_output_tiles(1)
-        early_finish(2)
-        ua.forward(0)
-        e1.zd()
+        dx_part(1)
         e2.ze()
-        s2.zc()
-        ub.forward(1)
-        s2.zd()
-        e1.ze()
-        s1.zg()
-        early_finish(3)
         late_finish(1)
         ub.forward(2)
-        s2.ze()
+        early_finish(3)
+        dx_sum(2)
         e1.zf()
+        dx_pass(2)
+        e1.zg()
+        late_finish(2)
         ua.forward(1)
+        e2.zf()
         ub.turn()
-        e1.zg()
+        s2.back(1)
+        s1.zg()
+        e2.zg()
         early_finish(4)
         ua.forward(2)
         ub.back(3)
+        dx_own()
+        s1.store()
         ua.turn()
-        dx_sum(2)
-        s2.zf()
-        dx_pass(2)
-        e1.back(1)
-        e2.zf()
-        dx_own()
+        dx_pass(3)
+        dx_sum(1)
+        dx_pass(1)
+        e2.back(1)
+        late_finish(3)
+        s2.store()
         ub.back(2)
-        late_finish(2)
         ua.back(3)
-        dx_sum(1)
-        s1.back(1)
-        s2.zg()
-        late_finish(3)
-        dx_pass(3)
-        ub.back(1)
-        dx_pass(1)
-        e2.zg()
-        s2.back(1)
-        s2.store()
         ua.back(2)
         dx_out()
-        s1.store()
-        e2.back(1)
+        ub.back(1)
+        e1.back(1)
+        e2.store()
+        e1.store()
         ua.back(1)
-        e1.store()
+        ub.store()
         ua.store()
-        e2.store()
-        ub.store()
-        r.small_out[...] = r.es[1]
-        r.late_out[...] = r.ls[0]
+        small_copies = (local(r.es.at[1], r.small_out), local(r.ls.at[0], r.late_out))
+        for copy in small_copies:
+            copy.start()
         oy_local.wait()
         oy_send.wait_recv()
         ig_local.wait()
         ig_send.wait_recv()
+        for copy in small_copies:
+            copy.wait()
         for unit in (s1, s2, e1, e2, ua, ub):
             unit.stored.wait()
         for p in range(HP):
@@ -970,8 +1023,8 @@
         us_out=((F, D), BF16, any_spec),
         ua_out=((D, 2 * W), BF16, any_spec),
         ub_out=((D, 2 * W), BF16, any_spec),
-        small_out=((8, D), F32, vmem_spec),
-        late_out=((8, W), F32, vmem_spec),
+        small_out=((8, D), F32, any_spec),
+        late_out=((8, W), F32, any_spec),
     )
     vm = lambda shape, kind: pltpu.VMEM(shape, kind)
     scratch = dict(
@@ -1024,6 +1077,10 @@
         ub=vm((D, 2 * W), BF16),
         s0=vm((D, D), BF16),
         e0=vm((2, D // 2, D), BF16),
+        z0=vm((3 * (D // 8), D), BF16),
+        z1=vm((2 * (D // 8), D), BF16),
+        z2=vm((D // 8, D), BF16),
+        z3=vm((D // 16, D), BF16),
         x0=vm((4, D // 4, D), BF16),
         l0=vm((4, 3 * (D // 16), D), BF16),
         l1=vm((4, 2 * (D // 16), D), BF16),
@@ -1070,18 +1127,39 @@
     reads = [pltpu.make_async_copy(p[0], p[1], r.sems.at[1 + k]) for k, p in enumerate(pieces)]
     for copy in reads:
         copy.start()
+    at_small = 2 * len(pieces) + 2
+    small_reads = [
+        pltpu.make_async_copy(r.small, r.small_v, r.sems.at[at_small]),
+        pltpu.make_async_copy(r.late, r.late_v, r.sems.at[at_small + 1]),
+    ]
+    for copy in small_reads:
+        copy.start()
     taken.wait()
     passed = pltpu.make_async_copy(r.out_v, r.out_out, r.sems.at[2 * len(pieces) + 1])
     passed.start()
-    small = r.small[...]
-    for name, at in (("fg", 0), ("fs", 1), ("sb", 2), ("ag", 3), ("as_", 4), ("ob", 5)):
-        getattr(r, name)[...] = small[at]
-    r.eb[0 : sh.width] = small[6]
-    r.eb[sh.width :] = small[7]
-    r.qb[...] = r.late[0]
-    r.vb[...] = r.late[1]
     writes = []
+
+    def vectors():
+        for copy in small_reads:
+            copy.wait()
+        for target, at in ((r.fg_v, 0), (r.fs_v, 1), (r.sb_v, 2), (r.ag_v, 3), (r.as_v, 4), (r.ob_v, 5)):
+            target[...] = r.small_v[at]
+        r.eb_v[0 : sh.width] = r.small_v[6]
+        r.eb_v[sh.width :] = r.small_v[7]
+        r.qb_v[...] = r.late_v[0]
+        r.vb_v[...] = r.late_v[1]
+        leaving = (
+            (r.fg_v, r.fg), (r.fs_v, r.fs), (r.sb_v, r.sb), (r.ag_v, r.ag), (r.as_v, r.as_), (r.ob_v, r.ob),
+            (r.eb_v, r.eb), (r.qb_v, r.qb), (r.vb_v, r.vb),
+        )
+        for k, (held, target) in enumerate(leaving):
+            copy = pltpu.make_async_copy(held, target, r.sems.at[at_small + 2 + k])
+            copy.start()
+            writes.append(copy)
+
     for k, (_, low, wide, target) in enumerate(pieces):
+        if k == 4:
+            vectors()
         reads[k].wait()
         rows = low.shape[0]
         step = 96 if rows % 96 == 0 else 64
@@ -1096,7 +1174,7 @@
         copy.start()
         writes.append(copy)
     passed.wait()
-    for copy in writes:
+    for k, copy in enumerate(writes):
         copy.wait()
 
 
@@ -1104,10 +1182,9 @@
     T, D, W, F = sh.tokens, sh.width, sh.hw, sh.units
     any_spec = pl.BlockSpec(memory_space=pl.ANY)
     hbm_spec = pl.BlockSpec(memory_space=pltpu.HBM)
-    vmem_spec = pl.BlockSpec(memory_space=pltpu.VMEM)
     ins = dict(
         out=hbm_spec, ig=hbm_spec, ue=hbm_spec, us=hbm_spec, ua=hbm_spec, ub=hbm_spec,
-        small=vmem_spec, late=vmem_spec,
+        small=hbm_spec, late=hbm_spec,
     )
     outs = dict(
         out_out=((T, D), BF16, any_spec),
@@ -1115,20 +1192,30 @@
         wq_out=((D, W), F32, any_spec),
         wk_out=((D, W), F32, any_spec),
         wv_out=((D, W), F32, any_spec),
-        qb=((W,), F32, vmem_spec),
-        vb=((W,), F32, vmem_spec),
+        qb=((W,), F32, any_spec),
+        vb=((W,), F32, any_spec),
         wo_out=((W, D), F32, any_spec),
-        ob=((D,), F32, vmem_spec),
-        ag=((D,), F32, vmem_spec),
-        as_=((D,), F32, vmem_spec),
+        ob=((D,), F32, any_spec),
+        ag=((D,), F32, any_spec),
+        as_=((D,), F32, any_spec),
         ue_out=((D, F), F32, any_spec),
-        eb=((F,), F32, vmem_spec),
+        eb=((F,), F32, any_spec),
         us_out=((F, D), F32, any_spec),
-        sb=((D,), F32, vmem_spec),
-        fg=((D,), F32, vmem_spec),
-        fs=((D,), F32, vmem_spec),
-    )
-    scratch = dict(sems=pltpu.SemaphoreType.DMA((24,)), out_v=pltpu.VMEM((T, D), BF16))
+        sb=((D,), F32, any_spec),
+        fg=((D,), F32, any_spec),
+        fs=((D,), F32, any_spec),
+    )
+    scratch = dict(
+        sems=pltpu.SemaphoreType.DMA((40,)),
+        out_v=pltpu.VMEM((T, D), BF16),
+        small_v=pltpu.VMEM((8, D), F32),
+        late_v=pltpu.VMEM((8, W), F32),
+        eb_v=pltpu.VMEM((F,), F32),
+    )
+    for name in ("fg_v", "fs_v", "sb_v", "ag_v", "as_v", "ob_v"):
+        scratch[name] = pltpu.VMEM((D,), F32)
+    for name in ("qb_v", "vb_v"):
+        scratch[name] = pltpu.VMEM((W,), F32)
     for low, wide, shape in (
         ("us_v", "usf", (2, F // 2, D)),
         ("ue_v", "uef", (2, W, F)),

time: 195 us -> 188 us (0.964)
  Pallas kernels: 194 us -> 186 us
    pallas_call x1, Pallas kernels: 184 us -> 176 us  [layer_call(): pl.pallas_call(make_kernel(sh, names), out_shape=[jax.ShapeDtypeStruct(o[...]
where the time goes in v4:
time: 188 us; the launch traced here: 187 us
  Pallas kernels  186 us (99%)
    pallas_call x1, Pallas kernels, layer_call(): pl.pallas_call(make_kernel(sh, names), out_shape=[jax.ShapeDtypeStruct(o[...  176 us
    pallas_call x1, Pallas kernels, finish_call(): pl.pallas_call(functools.partial(finish_kernel, sh, names), out_shape=[ja...  9.5 us

profile of v4, /device:TPU:0, one launch (start us, length us, event | category | flops | bytes accessed | tf_op | source)
XLA Modules:
  0.0 186.8 jit_solution(14467877657909956488)
XLA Ops:
  0.7 176.4 %layer.1 = (bf16[512,768]{1,0:T(8,128)(2,1)}, bf16[512,768]{1,0:T(8,128)(2,1)}, bf16[768,1536]{1,0:T(8,128)(2,1)}, bf16[1536,768]{1,0:T(8,128)(2,1)}, bf16[768,7...) custom-call(s32[1,512]{1,0:T(1,128)} %refs_0_.1, bf16[384]{0:T(512)(128)(2,1)} %refs_1_.1, ...), custom_call_target="tpu_custom_call" | custom-call | tf_op jit(solution)/shard_map/layer/pallas_call | solution.py:1094
  177.1 9.5 %finish.1 = (bf16[512,768]{1,0:T(8,128)(2,1)}, f32[512,768]{1,0:T(8,128)}, f32[768,384]{1,0:T(8,128)}, f32[768,384]{1,0:T(8,128)}, f32[768,384]{1,0:T(8,128)}, /...) custom-call(bf16[512,768]{1,0:T(8,128)(2,1)} %get-tuple-element.25.r, ...), custom_call_target="tpu_custom_call" | custom-call | tf_op jit(solution)/shard_map/finish/pallas_call | solution.py:1228

commit v5 on v4

--- a/solution.py
+++ b/solution.py
@@ -782,10 +782,17 @@
             dkv[rows, pl.ds(pl.multiple_of(p * 128, 128), 128)] = grad_k.astype(BF16)
             dkv[rows, pl.ds(pl.multiple_of(W + p * 128, 128), 128)] = grad_v.astype(BF16)
 
-        dx_y = [remote(r.xall.at[k, pl.ds(0, TM)], r.dxy.at[k], y_peer) for k in range(SLOTS)]
+        HR = TM // 2
+
+        def half(at, h):
+            return pl.ds(at + h * HR, HR)
+
+        dx_y = [
+            [remote(r.xall.at[k, half(0, h)], r.dxy.at[k, half(0, h)], y_peer) for h in range(2)] for k in range(SLOTS)
+        ]
 
         def dx_move(slot, target, peer):
-            return remote(r.xall.at[slot, pl.ds(TM, TM)], r.dxz.at[target], peer)
+            return [remote(r.xall.at[slot, half(TM, h)], r.dxz.at[target, half(0, h)], peer) for h in range(2)]
 
         dx_end = {3: dx_move(3, 0, z1_peer), 2: dx_move(2, 1, z1_peer), 1: dx_move(1, 2, z1_peer)}
         dx_mid = {3: dx_move(3, 3, z3_peer), 2: dx_move(2, 4, z3_peer), 1: dx_move(1, 5, z1_peer)}
@@ -796,43 +803,54 @@
 
         def dx_part(slot):
             r.xall[slot, 0:TM] = dx_rows(slot, peer_rows).astype(BF16)
-            go(dx_y[slot])
+            for h in range(2):
+                go(dx_y[slot][h])
             r.xall[slot, TM:] = dx_rows(slot, my_rows).astype(BF16)
 
-        def dx_sum(slot):
-            dx_y[slot].wait_recv()
-            total = r.xall[slot, TM:].astype(F32) + r.dxy[slot].astype(F32)
-            r.xall[slot, TM:] = total.astype(BF16)
-            go(dx_end[slot], is_end)
-
-        def dx_pass(slot):
-            came = {3: dx_end[2], 2: dx_end[3], 1: dx_mid[2]}[slot]
+        def add_to(slot, h, buf, at):
+            rows, kept = slice(h * HR, (h + 1) * HR), slice(TM + h * HR, TM + (h + 1) * HR)
+            total = r.xall[slot, kept].astype(F32) + buf[at, rows].astype(F32)
+            r.xall[slot, kept] = total.astype(BF16)
+
+        def dx_sum(slot, h):
+            dx_y[slot][h].wait_recv()
+            add_to(slot, h, r.dxy, slot)
+            go(dx_end[slot][h], is_end)
+
+        def dx_pass(slot, h):
+            came = {3: dx_end[2], 2: dx_end[3], 1: dx_mid[2]}[slot][h]
             at = {3: 1, 2: 0, 1: 4}[slot]
 
             @pl.when(is_mid)
             def _():
                 came.wait_recv()
-                total = r.xall[slot, TM:].astype(F32) + r.dxz[at].astype(F32)
-                r.xall[slot, TM:] = total.astype(BF16)
-
-            go(dx_mid[slot], is_mid)
-
-        def dx_last():
-            dx_y[0].wait_recv()
-            r.gmix[...] += r.dxy[0].astype(F32)
+                add_to(slot, h, r.dxz, at)
+
+            go(dx_mid[slot][h], is_mid)
+
+        ig_rows = [pl.ds(pl.multiple_of(t * TM + h * HR, HR), HR) for h in range(2)]
+        ig_local = [local(r.igm.at[half(0, h)], r.ig_out.at[ig_rows[h]]) for h in range(2)]
+        ig_send = [remote(r.igm.at[half(0, h)], r.ig_out.at[ig_rows[h]], y_peer) for h in range(2)]
+
+        def dx_out(h):
+            rows = slice(h * HR, (h + 1) * HR)
+            dx_y[0][h].wait_recv()
+            r.gmix[rows] += r.dxy[0, rows].astype(F32)
 
             @pl.when(is_mid)
             def _():
-                dx_end[1].wait_recv()
-                dx_mid[3].wait_recv()
-                r.gmix[...] += r.dxz[2].astype(F32) + r.dxz[3].astype(F32)
+                dx_end[1][h].wait_recv()
+                dx_mid[3][h].wait_recv()
+                r.gmix[rows] += r.dxz[2, rows].astype(F32) + r.dxz[3, rows].astype(F32)
 
             @pl.when(is_end)
             def _():
-                dx_mid[1].wait_recv()
-                r.gmix[...] += r.dxz[5].astype(F32)
-
-            r.igm[...] = r.gmix[...].astype(BF16)
+                dx_mid[1][h].wait_recv()
+                r.gmix[rows] += r.dxz[5, rows].astype(F32)
+
+            r.igm[rows] = r.gmix[rows].astype(BF16)
+            ig_local[h].start()
+            go(ig_send[h])
 
 
         def key_value_tiles(which):
@@ -853,16 +871,9 @@
 
         def dx_own():
             r.xall[0, 0:TM] = (dx_rows(0, peer_rows) + nt(r.dq[peer_rows, :], r.wqkv[:, :W])).astype(BF16)
-            go(dx_y[0])
+            for h in range(2):
+                go(dx_y[0][h])
             r.gmix[...] += dx_rows(0, my_rows) + nt(r.dq[my_rows, :], r.wqkv[:, :W])
-
-        ig_local = local(r.igm, r.ig_out.at[my_rows])
-        ig_send = remote(r.igm, r.ig_out.at[my_rows], y_peer)
-
-        def dx_out():
-            dx_last()
-            ig_local.start()
-            go(ig_send)
 
         shrink_tiles(0)
         s1.send(0)
@@ -872,128 +883,139 @@
         expand_tiles(0)
         e1.send(0)
         e2.send(0)
-        go(oy_send)
+        expand_tiles(1)
+        sum_blocks()
+        s2.forward(0)
         s1.add(0)
         s1.za()
-        expand_tiles(1)
-        sum_blocks()
-        early_start(0)
-        s2.forward(0)
         grad_heads()
-        e1.forward(0)
         set_bias(3)
-        run(lambda p: pull(3, p))
+
+        def beside_31():
+            e1.forward(0)
+
+        run(lambda p: pull(3, p), {1: beside_31})
+        dx_part(3)
+        s2.add(1)
+        s2.za()
         set_bias(2)
 
         def beside_20():
-            s2.add(1)
-            s2.za()
             s1.zb()
-            e2.forward(0)
 
         run(lambda p: pull(2, p), {0: beside_20})
+        e1.add(1)
+        e1.za()
+        e2.forward(0)
+        dx_part(2)
+        dx_sum(3, 0)
+        s2.zb()
         set_bias(1)
-
-        def beside_10():
-            e1.add(1)
-            e1.za()
-            early_finish(0)
-            s2.zb()
-
 
         def beside_11():
             s1.zc()
 
-        run(lambda p: pull(1, p), {0: beside_10, 1: beside_11})
+        run(lambda p: pull(1, p), {1: beside_11})
+        e1.zb()
         set_bias(0)
 
         def beside_00():
-            e1.zb()
-            early_finish(1)
-            s2.zc()
             e2.add(1)
             e2.za()
-            dx_part(3)
+            early_start(0)
             s1.zd()
+            s2.zc()
+            go(oy_send)
             s1.send(2)
 
-        run(lambda p: pull(0, p), {0: beside_00})
+
+        def beside_01():
+            s2.zd()
+            dx_sum(2, 0)
+            dx_pass(2, 0)
+            e1.zc()
+
+        run(lambda p: pull(0, p), {0: beside_00, 1: beside_01})
         s1.add(2)
         s1.spread(2)
         query_grads()
-        late_start(0)
-        e1.zc()
-        s2.zd()
-        e2.zb()
         key_value_tiles(0)
         ub.send(0)
+        e1.zd()
+        e2.zb()
+        dx_sum(3, 1)
+        s2.ze()
         s1.back(2)
         query_output_tiles(0)
         ua.send(0)
-        s2.ze()
-        e1.zd()
         key_value_tiles(1)
         ub.forward(0)
-        dx_sum(3)
+        early_finish(0)
         e2.zc()
+        early_finish(1)
+        late_start(0)
+        e1.ze()
+        s2.zf()
+        dx_pass(3, 0)
+        late_finish(0)
+        query_output_tiles(1)
+        ua.forward(0)
+        e2.zd()
+        ub.forward(1)
+        e2.ze()
+        e1.zf()
+        s2.zg()
+        early_finish(2)
+        ub.forward(2)
+        ua.forward(1)
+        ub.turn()
+        e1.zg()
+        e2.zf()
+        ua.forward(2)
+        dx_sum(2, 1)
+        dx_part(1)
+        dx_pass(2, 1)
+        dx_own()
+        ub.back(3)
+        late_finish(1)
+        ua.turn()
+        dx_sum(1, 0)
+        dx_pass(1, 0)
+        e2.zg()
+        ub.back(2)
         s1.ze()
-        e2.zd()
-        late_finish(0)
-        dx_part(2)
-        s2.zf()
-        query_output_tiles(1)
-        ub.forward(1)
-        early_finish(2)
-        e1.ze()
-        s2.zg()
-        ua.forward(0)
+        dx_pass(3, 1)
+        ua.back(3)
+        dx_out(0)
+        dx_sum(1, 1)
+        dx_pass(1, 1)
+        e1.back(1)
+        s2.back(1)
+        ua.back(2)
         s1.zf()
-        dx_part(1)
-        e2.ze()
-        late_finish(1)
-        ub.forward(2)
+        dx_out(1)
+        e2.back(1)
         early_finish(3)
-        dx_sum(2)
-        e1.zf()
-        dx_pass(2)
-        e1.zg()
+        ub.back(1)
+        ua.back(1)
+        s1.zg()
         late_finish(2)
-        ua.forward(1)
-        e2.zf()
-        ub.turn()
-        s2.back(1)
-        s1.zg()
-        e2.zg()
-        early_finish(4)
-        ua.forward(2)
-        ub.back(3)
-        dx_own()
-        s1.store()
-        ua.turn()
-        dx_pass(3)
-        dx_sum(1)
-        dx_pass(1)
-        e2.back(1)
-        late_finish(3)
-        s2.store()
-        ub.back(2)
-        ua.back(3)
-        ua.back(2)
-        dx_out()
-        ub.back(1)
-        e1.back(1)
         e2.store()
         e1.store()
-        ua.back(1)
+        late_finish(3)
         ub.store()
         ua.store()
+        s2.store()
+        early_finish(4)
+        s1.store()
         small_copies = (local(r.es.at[1], r.small_out), local(r.ls.at[0], r.late_out))
         for copy in small_copies:
             copy.start()
         oy_local.wait()
         oy_send.wait_recv()
-        ig_local.wait()
-        ig_send.wait_recv()
+        for h in range(2):
+            ig_local[h].wait()
+            ig_send[h].wait_recv()
         for copy in small_copies:
             copy.wait()
         for unit in (s1, s2, e1, e2, ua, ub):
@@ -1028,9 +1050,9 @@
     )
     vm = lambda shape, kind: pltpu.VMEM(shape, kind)
     scratch = dict(
-        send=pltpu.SemaphoreType.DMA((160,)),
-        recv=pltpu.SemaphoreType.DMA((160,)),
-        local=pltpu.SemaphoreType.DMA((24,)),
+        send=pltpu.SemaphoreType.DMA((192,)),
+        recv=pltpu.SemaphoreType.DMA((192,)),
+        local=pltpu.SemaphoreType.DMA((32,)),
         xall=vm((4, T, D), BF16),
         xt=vm((D, 4 * T), BF16),
         wqkv=vm((D, 3 * W), BF16),

time: 188 us -> 184 us (0.979)
  Pallas kernels: 186 us -> 183 us
    pallas_call x1, Pallas kernels: 176 us -> 174 us  [layer_call(): pl.pallas_call(make_kernel(sh, names), out_shape=[jax.ShapeDtypeStruct(o[...]
where the time goes in v5:
time: 184 us
  Pallas kernels  183 us (99%)
    pallas_call x1, Pallas kernels, layer_call(): pl.pallas_call(make_kernel(sh, names), out_shape=[jax.ShapeDtypeStruct(o[...  174 us
    pallas_call x1, Pallas kernels, finish_call(): pl.pallas_call(functools.partial(finish_kernel, sh, names), out_shape=[ja...  9.5 us

profile of v5, /device:TPU:0, one launch (start us, length us, event | category | flops | bytes accessed | tf_op | source)
XLA Modules:
  0.0 184.2 jit_solution(8835219993868249014)
XLA Ops:
  0.7 173.8 %layer.1 = (bf16[512,768]{1,0:T(8,128)(2,1)}, bf16[512,768]{1,0:T(8,128)(2,1)}, bf16[768,1536]{1,0:T(8,128)(2,1)}, bf16[1536,768]{1,0:T(8,128)(2,1)}, bf16[768,7...) custom-call(s32[1,512]{1,0:T(1,128)} %refs_0_.1, bf16[384]{0:T(512)(128)(2,1)} %refs_1_.1, ...), custom_call_target="tpu_custom_call" | custom-call | tf_op jit(solution)/shard_map/layer/pallas_call | solution.py:1116
  174.5 9.5 %finish.1 = (bf16[512,768]{1,0:T(8,128)(2,1)}, f32[512,768]{1,0:T(8,128)}, f32[768,384]{1,0:T(8,128)}, f32[768,384]{1,0:T(8,128)}, f32[768,384]{1,0:T(8,128)}, /...) custom-call(bf16[512,768]{1,0:T(8,128)(2,1)} %get-tuple-element.25.r, ...), custom_call_target="tpu_custom_call" | custom-call | tf_op jit(solution)/shard_map/finish/pallas_call | solution.py:1250

commit v6 on v5

--- a/solution.py
+++ b/solution.py
@@ -70,7 +70,7 @@
     TILE = 512
     NTILE = F // TILE
     SLOTS = 4
-    PARTS = 2
+    PARTS = 4
     PR = TM // PARTS
 
     def kernel(*refs):
@@ -394,68 +394,71 @@
 
         go(w_y[0])
         go(w_y[1])
+        arrive(1, 0)
+        hop1(0)
         project()
-        arrive(1, 0)
 
         def with_00():
             go(w_y[2])
-            go(w_y[3])
-            hop1(0)
-            arrive(1, 1)
-            arrive(2, 0)
-            hop2(0)
+
+
+        def with_01():
             hop1(1)
 
-
-        def with_01():
-            arrive(2, 1)
-
         run(lambda p: attend(slots[0], p), {0: with_00, 1: with_01})
-        arrive(3, 0)
-        hop2(1)
+        arrive(1, 1)
+        arrive(1, 2)
+        arrive(1, 3)
+        hop2(0)
+        go(w_y[3])
+        arrive(2, 0)
+        arrive(2, 1)
+        arrive(2, 2)
+        arrive(2, 3)
         next_block(1)
+        hop1(2)
+
+        def with_10():
+            arrive(3, 0)
+
 
         def with_11():
+            hop2(1)
             arrive(3, 1)
-            hop1(2)
-            go(w_y[4])
-            hop3(0)
-
-        run(lambda p: attend(slots[1], p), {1: with_11})
+
+        run(lambda p: attend(slots[1], p), {0: with_10, 1: with_11})
+        flip_inputs(slots[1])
+        arrive(3, 2)
+        hop2(2)
+        hop3(0)
+        next_block(2)
+        arrive(3, 3)
+        go(w_y[4])
         hop1(3)
-        next_block(2)
-
-        def with_20():
-            hop3(1)
-
-
-        def with_21():
-            hop2(2)
-
-        run(lambda p: attend(slots[2], p), {0: with_20, 1: with_21})
+        run(lambda p: attend(slots[2], p))
+        next_block(3)
         hop2(3)
-        weights_done(0)
-        next_block(3)
         attend_last(0)
         hop1(4)
         attend_last(1)
+        hop3(1)
         attend_last(2)
-        flip_inputs(slots[1])
+        hop3(2)
         hop2(4)
+        hop3(3)
+        weights_done(0)
         out_project()
         first_norm()
-        hop3(2)
+        weights_done(1)
+        flip_inputs(slots[0])
+        weights_done(2)
+        hop3(4)
+        weights_done(3)
+        own_units()
+        weights_done(4)
+        other_units()
         flip_inputs(slots[2])
         flip_inputs(slots[3])
-        weights_done(1)
-        hop3(3)
-        weights_done(2)
-        flip_inputs(slots[0])
-        hop3(4)
-        own_units()
-        weights_done(3)
-        weights_done(4)
-        other_units()
         loads.cot.wait()
         normed2, recip2 = normalise(r.sec[...])
         upstream = r.cot[...].astype(F32)
@@ -883,130 +886,127 @@
         expand_tiles(0)
         e1.send(0)
         e2.send(0)
+        s1.add(0)
+        s1.za()
+        s2.forward(0)
+        go(oy_send)
         expand_tiles(1)
         sum_blocks()
-        s2.forward(0)
-        s1.add(0)
-        s1.za()
         grad_heads()
+        e1.forward(0)
         set_bias(3)
 
         def beside_31():
-            e1.forward(0)
+            e2.forward(0)
 
         run(lambda p: pull(3, p), {1: beside_31})
-        dx_part(3)
         s2.add(1)
         s2.za()
+        s1.zb()
+        dx_part(3)
         set_bias(2)
 
-        def beside_20():
-            s1.zb()
-
-        run(lambda p: pull(2, p), {0: beside_20})
-        e1.add(1)
-        e1.za()
-        e2.forward(0)
+        def beside_21():
+            e1.add(1)
+            e1.za()
+
+        run(lambda p: pull(2, p), {1: beside_21})
+        s2.zb()
         dx_part(2)
         dx_sum(3, 0)
-        s2.zb()
+        early_start(0)
+        s1.zc()
         set_bias(1)
 
         def beside_11():
-            s1.zc()
-
-        run(lambda p: pull(1, p), {1: beside_11})
-        e1.zb()
-        set_bias(0)
-
-        def beside_00():
+            s2.zc()
+            e1.zb()
             e2.add(1)
             e2.za()
-            early_start(0)
-            s1.zd()
-            s2.zc()
-            go(oy_send)
-            s1.send(2)
-
-
-        def beside_01():
+
+        run(lambda p: pull(1, p), {1: beside_11})
+        set_bias(0)
+
+        def beside_00():
             s2.zd()
             dx_sum(2, 0)
             dx_pass(2, 0)
-            e1.zc()
-
-        run(lambda p: pull(0, p), {0: beside_00, 1: beside_01})
+            s1.zd()
+            s1.send(2)
+
+        run(lambda p: pull(0, p), {0: beside_00})
         s1.add(2)
         s1.spread(2)
         query_grads()
+        e2.zb()
+        e1.zc()
         key_value_tiles(0)
         ub.send(0)
-        e1.zd()
-        e2.zb()
-        dx_sum(3, 1)
-        s2.ze()
-        s1.back(2)
         query_output_tiles(0)
         ua.send(0)
+        early_finish(0)
+        s1.back(2)
+        s2.ze()
         key_value_tiles(1)
         ub.forward(0)
-        early_finish(0)
+        e1.zd()
+        query_output_tiles(1)
+        dx_pass(3, 0)
         e2.zc()
+        s2.zf()
+        dx_sum(3, 1)
+        dx_own()
+        e1.ze()
+        late_start(0)
+        late_finish(0)
+        e2.zd()
+        ua.forward(0)
+        ub.forward(1)
+        e1.zf()
+        late_finish(1)
+        e2.ze()
+        ub.forward(2)
+        ua.forward(1)
         early_finish(1)
-        late_start(0)
-        e1.ze()
-        s2.zf()
-        dx_pass(3, 0)
-        late_finish(0)
-        query_output_tiles(1)
-        ua.forward(0)
-        e2.zd()
-        ub.forward(1)
-        e2.ze()
-        e1.zf()
+        e1.zg()
+        ub.turn()
         s2.zg()
         early_finish(2)
-        ub.forward(2)
-        ua.forward(1)
-        ub.turn()
-        e1.zg()
         e2.zf()
+        dx_part(1)
         ua.forward(2)
         dx_sum(2, 1)
-        dx_part(1)
+        ub.back(3)
         dx_pass(2, 1)
-        dx_own()
-        ub.back(3)
-        late_finish(1)
         ua.turn()
+        s1.ze()
+        e2.zg()
         dx_sum(1, 0)
         dx_pass(1, 0)
-        e2.zg()
         ub.back(2)
-        s1.ze()
-        dx_pass(3, 1)
         ua.back(3)
-        dx_out(0)
+        e1.back(1)
         dx_sum(1, 1)
         dx_pass(1, 1)
-        e1.back(1)
+        s1.zf()
+        ua.back(2)
+        dx_pass(3, 1)
+        e1.store()
+        early_finish(3)
+        dx_out(0)
+        e2.back(1)
         s2.back(1)
-        ua.back(2)
-        s1.zf()
         dx_out(1)
-        e2.back(1)
-        early_finish(3)
+        late_finish(2)
         ub.back(1)
         ua.back(1)
+        s2.store()
         s1.zg()
-        late_finish(2)
+        early_finish(4)
+        ua.store()
         e2.store()
-        e1.store()
         late_finish(3)
         ub.store()
-        ua.store()
-        s2.store()
-        early_finish(4)
         s1.store()
         small_copies = (local(r.es.at[1], r.small_out), local(r.ls.at[0], r.late_out))
         for copy in small_copies:
@@ -1050,8 +1050,8 @@
     )
     vm = lambda shape, kind: pltpu.VMEM(shape, kind)
     scratch = dict(
-        send=pltpu.SemaphoreType.DMA((192,)),
-        recv=pltpu.SemaphoreType.DMA((192,)),
+        send=pltpu.SemaphoreType.DMA((224,)),
+        recv=pltpu.SemaphoreType.DMA((224,)),
         local=pltpu.SemaphoreType.DMA((32,)),
         xall=vm((4, T, D), BF16),
         xt=vm((D, 4 * T), BF16),

time: 184 us -> 183 us (level)
  Pallas kernels: 183 us -> 181 us
    pallas_call x1, Pallas kernels: 174 us -> 172 us  [layer_call(): pl.pallas_call(make_kernel(sh, names), out_shape=[jax.ShapeDtypeStruct(o[...]
where the time goes in v6:
time: 183 us; the launch traced here: 182 us
  Pallas kernels  181 us (99%)
    pallas_call x1, Pallas kernels, layer_call(): pl.pallas_call(make_kernel(sh, names), out_shape=[jax.ShapeDtypeStruct(o[...  172 us
    pallas_call x1, Pallas kernels, finish_call(): pl.pallas_call(functools.partial(finish_kernel, sh, names), out_shape=[ja...  9.5 us

profile of v6, /device:TPU:0, one launch (start us, length us, event | category | flops | bytes accessed | tf_op | source)
XLA Modules:
  0.0 182.1 jit_solution(5937033623276396087)
XLA Ops:
  0.7 171.8 %layer.1 = (bf16[512,768]{1,0:T(8,128)(2,1)}, bf16[512,768]{1,0:T(8,128)(2,1)}, bf16[768,1536]{1,0:T(8,128)(2,1)}, bf16[1536,768]{1,0:T(8,128)(2,1)}, bf16[768,7...) custom-call(s32[1,512]{1,0:T(1,128)} %refs_0_.1, bf16[384]{0:T(512)(128)(2,1)} %refs_1_.1, ...), custom_call_target="tpu_custom_call" | custom-call | tf_op jit(solution)/shard_map/layer/pallas_call | solution.py:1116
  172.4 9.5 %finish.1 = (bf16[512,768]{1,0:T(8,128)(2,1)}, f32[512,768]{1,0:T(8,128)}, f32[768,384]{1,0:T(8,128)}, f32[768,384]{1,0:T(8,128)}, f32[768,384]{1,0:T(8,128)}, /...) custom-call(bf16[512,768]{1,0:T(8,128)(2,1)} %get-tuple-element.25.r, ...), custom_call_target="tpu_custom_call" | custom-call | tf_op jit(solution)/shard_map/finish/pallas_call | solution.py:1250

commit v7 on v6

--- a/solution.py
+++ b/solution.py
@@ -127,6 +127,14 @@
                 else:
                     pl.when(where)(lambda copy=copy: copy.wait_send())
             unsent[:] = kept
+
+        def wait_first(count):
+            for copy, where in unsent[:count]:
+                if where is None:
+                    copy.wait_send()
+                else:
+                    pl.when(where)(lambda copy=copy: copy.wait_send())
+            del unsent[:count]
 
         loads = types.SimpleNamespace(
             x=local(r.x_in, r.xall.at[0]),
@@ -995,6 +1003,7 @@
         early_finish(3)
         dx_out(0)
         e2.back(1)
+        old_sends = len(unsent)
         s2.back(1)
         dx_out(1)
         late_finish(2)
@@ -1003,6 +1012,7 @@
         s2.store()
         s1.zg()
         early_finish(4)
+        wait_first(old_sends)
         ua.store()
         e2.store()
         late_finish(3)

time: 183 us -> 182 us (level)
  no operation moved by 1% of the time
where the time goes in v7:
time: 182 us
  Pallas kernels  181 us (99%)
    pallas_call x1, Pallas kernels, layer_call(): pl.pallas_call(make_kernel(sh, names), out_shape=[jax.ShapeDtypeStruct(o[...  172 us
    pallas_call x1, Pallas kernels, finish_call(): pl.pallas_call(functools.partial(finish_kernel, sh, names), out_shape=[ja...  9.5 us

profile of v7, /device:TPU:0, one launch (start us, length us, event | category | flops | bytes accessed | tf_op | source)
XLA Modules:
  0.0 182.0 jit_solution(13338725882133090523)
XLA Ops:
  0.7 171.7 %layer.1 = (bf16[512,768]{1,0:T(8,128)(2,1)}, bf16[512,768]{1,0:T(8,128)(2,1)}, bf16[768,1536]{1,0:T(8,128)(2,1)}, bf16[1536,768]{1,0:T(8,128)(2,1)}, bf16[768,7...) custom-call(s32[1,512]{1,0:T(1,128)} %refs_0_.1, bf16[384]{0:T(512)(128)(2,1)} %refs_1_.1, ...), custom_call_target="tpu_custom_call" | custom-call | tf_op jit(solution)/shard_map/layer/pallas_call | solution.py:1126
  172.4 9.5 %finish.1 = (bf16[512,768]{1,0:T(8,128)(2,1)}, f32[512,768]{1,0:T(8,128)}, f32[768,384]{1,0:T(8,128)}, f32[768,384]{1,0:T(8,128)}, f32[768,384]{1,0:T(8,128)}, /...) custom-call(bf16[512,768]{1,0:T(8,128)(2,1)} %get-tuple-element.25.r, ...), custom_call_target="tpu_custom_call" | custom-call | tf_op jit(solution)/shard_map/finish/pallas_call | solution.py:1260
